TPU v7x, 1024 devices: a whole 4x8x16 slice. The times are simulated.
1024 devices in a mesh: dp: 16 (over z), expert: 16 (over y, core), tensor: 4 (over x).
Axes of the slice: x: 4, y: 8, z: 16, core: 2. Of those that a mesh axis runs over, the one named last changes fastest.
Arguments:
- tokens: bfloat16 [4096, 2048], P(('dp', 'expert', 'tensor')), may hold values from -6 to 6
- routes: int32 [4096, 6], P(('dp', 'expert')), may hold values from 0 to 15, as said below
- positions: int32 [4096, 6], P(('dp', 'expert')), may hold values from 0 to 7, as said below
- combine_weights: float32 [4096, 6], P(('dp', 'expert')), may hold values from 0.1 to 1
- cotangent: bfloat16 [4096, 2048], P(('dp', 'expert', 'tensor')), may hold values from -6 to 6
- gate_weight: bfloat16 [16, 2048, 1408], P('expert', None, 'tensor'), may hold values from -0.125 to 0.125
- up_weight: bfloat16 [16, 2048, 1408], P('expert', None, 'tensor'), may hold values from -0.125 to 0.125
- down_weight: bfloat16 [16, 2048, 1408], P('expert', None, 'tensor'), may hold values from -0.15625 to 0.15625
Outputs:
- layer_out: bfloat16 [4096, 2048], P(('dp', 'expert', 'tensor'))
- grad_tokens: bfloat16 [4096, 2048], P(('dp', 'expert', 'tensor'))
- grad_down: bfloat16 [16, 2048, 1408], P('expert', 'dp', 'tensor')
Inputs may be any that keep to these rules, and one draw needn't show every extreme that they name: `routes`: each row names 6 different experts. Within each aligned block of 16 rows, no expert is named by more than 8 rows, and one expert, the same in every block, is named by exactly 8 rows. `positions`: within each aligned block of 16 rows, no two choices share both expert and position.
All inputs are finite; a program needn't handle non-finite values.
Results may differ from a plain program's by a relative error of at most 0.017.
Values may be sent and summed in bfloat16 or wider, within the bound.
A program may use at most 32 MiB of HBM per device.

v0:
```python
import jax
import jax.numpy as jnp
from jax import lax
from jax.sharding import PartitionSpec as P


def outer_term(left, right):
    return jnp.einsum("erd,erf->edf", left, right, preferred_element_type=jnp.float32)


def shards(
    tokens, routes, positions, combine_weights, cotangent, gate_weight, up_weight, down_weight
):
    experts_here = gate_weight.shape[0]
    experts_all = experts_here * lax.axis_size("expert")
    replicas = lax.axis_size("dp")
    group_size = routes.shape[0]
    capacity = group_size // 2
    slot_count = experts_all * capacity
    slot_ids = routes * capacity + positions
    slot_range = jnp.arange(slot_count, dtype=jnp.int32)
    matches = slot_ids[:, :, None] == slot_range
    chooser = matches.astype(jnp.bfloat16)
    scatter_table = jnp.any(slot_range[:, None, None] == slot_ids[None, :, :], axis=2).astype(
        jnp.bfloat16
    )
    slot_gain = jnp.sum(jnp.where(matches, combine_weights[:, :, None], 0.0), axis=(0, 1))

    def fill_slots(rows_block, gain):
        picked = jnp.dot(scatter_table, rows_block, preferred_element_type=jnp.float32)
        if gain is not None:
            picked = picked * gain[:, None]
        return picked.astype(jnp.bfloat16).reshape(experts_all, capacity, rows_block.shape[1])

    def dispatch(rows, gain):
        gathered = lax.all_gather(rows, "tensor", axis=0, tiled=True)
        return lax.all_to_all(
            fill_slots(gathered, gain), "expert", split_axis=0, concat_axis=1, tiled=True
        )

    def gather_back(partial_slots, weights):
        returned = lax.all_to_all(partial_slots, "expert", split_axis=1, concat_axis=0, tiled=True)
        flattened = returned.reshape(slot_count, returned.shape[2])
        picked = jnp.einsum("tks,sd->tkd", chooser, flattened, preferred_element_type=jnp.float32)
        if weights is not None:
            picked = picked * weights[:, :, None]
        summed = jnp.sum(picked, axis=1)
        return lax.psum_scatter(
            summed.astype(jnp.bfloat16), "tensor", scatter_dimension=0, tiled=True
        ).astype(jnp.float32)

    expert_rows = dispatch(tokens, None)
    gate_pre = jnp.einsum(
        "erd,edf->erf", expert_rows, gate_weight, preferred_element_type=jnp.float32
    )
    up_pre = jnp.einsum("erd,edf->erf", expert_rows, up_weight, preferred_element_type=jnp.float32)
    squash = jax.nn.sigmoid(gate_pre)
    swish = gate_pre * squash
    activation = (swish * up_pre).astype(jnp.bfloat16)
    expert_part = jnp.einsum(
        "erf,edf->erd", activation, down_weight, preferred_element_type=jnp.float32
    ).astype(jnp.bfloat16)
    layer_out = gather_back(expert_part, combine_weights).astype(jnp.bfloat16)
    slot_grads = dispatch(cotangent, slot_gain)
    act_grad = jnp.einsum(
        "erd,edf->erf", slot_grads, down_weight, preferred_element_type=jnp.float32
    )
    gate_back = (act_grad * up_pre * squash * (1.0 + gate_pre * (1.0 - squash))).astype(
        jnp.bfloat16
    )
    up_back = (act_grad * swish).astype(jnp.bfloat16)
    input_gate = jnp.einsum(
        "erf,edf->erd", gate_back, gate_weight, preferred_element_type=jnp.float32
    )
    input_up = jnp.einsum("erf,edf->erd", up_back, up_weight, preferred_element_type=jnp.float32)
    input_part = (input_gate + input_up).astype(jnp.bfloat16)
    grad_tokens = gather_back(input_part, None).astype(jnp.bfloat16)
    total = lax.psum_scatter(
        outer_term(slot_grads, activation).astype(jnp.bfloat16),
        "dp",
        scatter_dimension=1,
        tiled=True,
    ).astype(jnp.float32)
    grad_down = (total * (1.0 / replicas)).astype(jnp.bfloat16)
    return (layer_out, grad_tokens, grad_down)


def solution(mesh):
    return jax.shard_map(
        shards,
        mesh=mesh,
        in_specs=(
            P(("dp", "expert", "tensor"), None),
            P(("dp", "expert"), None),
            P(("dp", "expert"), None),
            P(("dp", "expert"), None),
            P(("dp", "expert", "tensor"), None),
            P("expert", None, "tensor"),
            P("expert", None, "tensor"),
            P("expert", None, "tensor"),
        ),
        out_specs=(
            P(("dp", "expert", "tensor"), None),
            P(("dp", "expert", "tensor"), None),
            P("expert", "dp", "tensor"),
        ),
        check_vma=False,
    )
```

profile of v0, /device:TPU:6, one launch (start us, length us, event | category | flops | bytes accessed | tf_op | source)
XLA Modules:
  0.0 211.3 jit_solution(88066172117676612)
XLA Ops:
  8.0 0.0 copy-start
  8.0 0.0 copy-start.10
  8.0 0.0 copy-start.11
  8.0 0.8 multiply_add_fusion
  8.8 0.1 fusion.28
  8.9 22.0 %all-gather = bf16[4,4,2048]{2,1,0:T(4,128)(2,1)S(1)} all-gather(bf16[1,4,2048]{2,1,0:T(4,128)(2,1)} %bitcast.75), channel_id=1, replica_groups=mesh['dp'=16,'expert'=16,'tensor'=4] {'tensor'}, dimensions={0}, use_global_device_ids=true | all-gather | bytes 81920 | tf_op jit(solution)/shard_map/all_gather | solution.py:36
  31.0 1.1 fusion.6
  32.1 3.7 %all-to-all-start = ((bf16[16,8,2048]{2,1,0:T(8,128)(2,1)}), bf16[16,8,2048]{2,1,0:T(8,128)(2,1)S(1)}, u32[]{:S(2)}, u32[]{:S(2)}) async-start(bf16[16,8,2048]{2,1,0:T(8,128)(2,1)} %fusion.6), calls=%async_computation | async-start | bytes 1048576 | tf_op jit(solution)/shard_map/all_to_all | solution.py:37
  35.8 0.0 copy-done.10
  35.8 11.9 %all-gather.1 = bf16[4,4,2048]{2,1,0:T(4,128)(2,1)S(1)} all-gather(bf16[1,4,2048]{2,1,0:T(4,128)(2,1)S(1)} %bitcast.76), channel_id=1, replica_groups=mesh['dp'=16,'expert'=16,'tensor'=4] {'tensor'}, dimensions={0}, use_global_device_ids=true | all-gather | bytes 81920 | tf_op jit(solution)/shard_map/all_gather | solution.py:36
  47.7 0.0 copy-done.11
  47.7 0.1 select_reduce_fusion
  47.8 1.2 fusion.3
  49.0 2.7 %all-to-all-done = bf16[16,8,2048]{2,1,0:T(8,128)(2,1)S(1)} async-done(((bf16[16,8,2048]{2,1,0:T(8,128)(2,1)}), bf16[16,8,2048]{2,1,0:T(8,128)(2,1)S(1)}, u32[]{:S(2)}, u32[]{:S(2)}) %all-to-all-start) | async-done | bytes 524320 | tf_op jit(solution)/shard_map/all_to_all | solution.py:37
  51.7 0.8 copy-done.4
  52.5 4.4 %all-to-all-start.2 = ((bf16[16,8,2048]{2,1,0:T(8,128)(2,1)}), bf16[16,8,2048]{2,1,0:T(8,128)(2,1)S(1)}, u32[]{:S(2)}, u32[]{:S(2)}) async-start(bf16[16,8,2048]{2,1,0:T(8,128)(2,1)} %fusion.3), calls=%async_computation.2 | async-start | bytes 1048576 | tf_op jit(solution)/shard_map/all_to_all | solution.py:37
  56.9 0.0 copy-done.2
  56.9 0.0 copy-start.5
  57.0 1.6 fusion.15
  58.6 0.0 copy-done
  58.6 0.0 copy-done.5
  58.6 0.0 copy-start.6
  58.6 0.0 copy-start.1
  58.6 1.2 multiply_convert_fusion.3
  59.9 0.0 copy-done.6
  59.9 0.6 copy-done.8
  60.5 0.5 fusion.4
  61.0 1.8 copy.38
  62.8 0.5 broadcast.22
  63.3 5.6 %reduce = bf16[128,2048]{1,0:T(8,128)(2,1)} reduce(bf16[128,1,2048]{2,1,0:T(2,128)(2,1)} %bitcast.71, bf16[]{:T(256)} %broadcast.22), dimensions={1}, to_apply=%bitcast.68.reduce_sub_computation | reduce | bytes 1048578
  68.8 2.4 %reshape.117 = bf16[16,2,8192]{2,1,0:T(2,128)(2,1)} reshape(bf16[128,2048]{1,0:T(8,128)(2,1)} %reduce) | data formatting | bytes 1048576
  71.2 1.9 all-to-all-done.2
  73.1 5.4 %all-to-all-start.1 = ((bf16[16,2,8192]{2,1,0:T(2,128)(2,1)}), bf16[16,2,8192]{2,1,0:T(2,128)(2,1)}, u32[]{:S(2)}, u32[]{:S(2)}) async-start(bf16[16,2,8192]{2,1,0:T(2,128)(2,1)} %reshape.117), calls=%async_computation.1 | async-start | bytes 1048576 | tf_op jit(solution)/shard_map/all_to_all | solution.py:42
  78.5 0.0 copy-start.3
  78.5 0.5 fusion.7
  79.1 0.8 copy-done.3
  79.9 0.0 copy-done.7
  79.9 0.0 copy-done.9
  79.9 0.5 fusion.13
  80.4 0.5 fusion.5
  81.0 0.8 copy.37
  81.8 3.7 %reduce.1 = bf16[128,2048]{1,0:T(8,128)(2,1)S(1)} reduce(bf16[128,1,2048]{2,1,0:T(2,128)(2,1)S(1)} %bitcast.72, bf16[]{:T(256)} %broadcast.22), dimensions={1}, to_apply=%bitcast.67.reduce_sub_computation | reduce | bytes 1048578
  85.5 1.3 reshape.119
  86.8 7.6 %all-to-all-done.1 = bf16[16,2,8192]{2,1,0:T(2,128)(2,1)} async-done(((bf16[16,2,8192]{2,1,0:T(2,128)(2,1)}), bf16[16,2,8192]{2,1,0:T(2,128)(2,1)}, u32[]{:S(2)}, u32[]{:S(2)}) %all-to-all-start.1) | async-done | bytes 524320 | tf_op jit(solution)/shard_map/all_to_all | solution.py:42
  94.5 4.2 %all-to-all-start.3 = ((bf16[16,2,8192]{2,1,0:T(2,128)(2,1)}), bf16[16,2,8192]{2,1,0:T(2,128)(2,1)S(1)}, u32[]{:S(2)}, u32[]{:S(2)}) async-start(bf16[16,2,8192]{2,1,0:T(2,128)(2,1)} %reshape.119), calls=%async_computation.3 | async-start | bytes 1048576 | tf_op jit(solution)/shard_map/all_to_all | solution.py:42
  98.7 0.0 all-reduce.5.cloned.1.call-start
  98.8 2.2 %reshape.118 = bf16[128,1,2048]{2,1,0:T(2,128)(2,1)S(1)} reshape(bf16[16,2,8192]{2,1,0:T(2,128)(2,1)} %all-to-all-done.1) | data formatting | bytes 1048576
  101.0 1.1 fusion.17
  102.1 12.8 %all-to-all-done.3 = bf16[16,2,8192]{2,1,0:T(2,128)(2,1)S(1)} async-done(((bf16[16,2,8192]{2,1,0:T(2,128)(2,1)}), bf16[16,2,8192]{2,1,0:T(2,128)(2,1)S(1)}, u32[]{:S(2)}, u32[]{:S(2)}) %all-to-all-start.3) | async-done | bytes 524320 | tf_op jit(solution)/shard_map/all_to_all | solution.py:42
  114.9 0.5 reshape.120
  115.4 1.1 convolution_reduce_fusion
  116.5 0.0 all-reduce.5.cloned.1.call-update
  116.6 0.0 reduce-scatter.4.cloned.1.call-start
  116.6 1.4 fusion
  118.0 5.8 %copy.20 = bf16[1,2048,352]{2,0,1:T(2,128)(2,1)} copy(bf16[1,2048,352]{1,2,0:T(8,128)(2,1)S(1)} %fusion) | data formatting | bytes 2883584
  123.8 3.3 %copy.36 = bf16[2048,1,352]{2,0,1:T(8,128)(2,1)} copy(bf16[2048,1,352]{2,1,0:T(2,128)(2,1)} %bitcast.69) | data formatting | bytes 2883584
  127.1 0.0 reduce-scatter.4.cloned.1.call-update
  127.2 1.3 dynamic-slice
  129.1 49.0 %all-reduce.5.cloned.1.call-done = (bf16[16,2048]{1,0:T(8,128)(2,1)}, bf16[16,2048]{1,0:T(8,128)(2,1)}) async-done(((bf16[16,2048]{1,0:T(8,128)(2,1)}, bf16[16,2048]{1,0:T(8,128)(2,1)}), (bf16[16,2048]{1,0:T(8,128)(2,1)}, bf16[16,2048]{1,0:T(8,128)(2,1)})) %all-reduce.5.cloned.1.call-update) | async-done | bytes 131088
  178.1 1.4 constant_dynamic-slice_fusion
  179.6 22.5 %reduce-scatter.4.cloned.1.call-done = bf16[128,352]{1,0:T(8,128)(2,1)} async-done(((bf16[2048,352]{1,0:T(8,128)(2,1)}), bf16[128,352]{1,0:T(8,128)(2,1)}) %reduce-scatter.4.cloned.1.call-update) | async-done | bytes 90128
  202.0 1.0 reshape_bitcast_fusion
  203.0 0.2 copy.21
  203.2 0.7 multiply_convert_fusion
  (8 shorter events, 0.1 us)
Async XLA Ops:
  8.0 50.6 %copy-start = (bf16[1,2048,352]{1,2,0:T(8,128)(2,1)S(1)}, bf16[1,2048,352]{1,2,0:T(8,128)(2,1)}, u32[]{:S(2)}) copy-start(bf16[1,2048,352]{1,2,0:T(8,128)(2,1)} %param.14) | copy-start | bytes 4325380
  8.0 27.8 %copy-start.10 = (bf16[4,2048]{1,0:T(4,128)(2,1)S(1)}, bf16[4,2048]{1,0:T(4,128)(2,1)}, u32[]{:S(2)}) copy-start(bf16[4,2048]{1,0:T(4,128)(2,1)} %param.12) | copy-start | bytes 49156
  8.0 39.7 %copy-start.11 = (f32[16,6]{0,1:T(8,128)S(1)}, f32[16,6]{0,1:T(8,128)}, u32[]{:S(2)}) copy-start(f32[16,6]{0,1:T(8,128)} %param.11) | copy-start | bytes 1156
  32.1 24.8 %copy-start.2 = (bf16[1,2048,352]{1,2,0:T(8,128)(2,1)S(1)}, bf16[1,2048,352]{1,2,0:T(8,128)(2,1)}, u32[]{:S(2)}) copy-start(bf16[1,2048,352]{1,2,0:T(8,128)(2,1)} %param.13) | copy-start | bytes 4325380
  32.1 19.6 %all-to-all-start = ((bf16[16,8,2048]{2,1,0:T(8,128)(2,1)}), bf16[16,8,2048]{2,1,0:T(8,128)(2,1)S(1)}, u32[]{:S(2)}, u32[]{:S(2)}) async-start(bf16[16,8,2048]{2,1,0:T(8,128)(2,1)} %fusion.6), calls=%async_computation | async-start | bytes 1048576 | tf_op jit(solution)/shard_map/all_to_all | solution.py:37
  51.7 0.8 copy-start.4
  52.5 20.6 %all-to-all-start.2 = ((bf16[16,8,2048]{2,1,0:T(8,128)(2,1)}), bf16[16,8,2048]{2,1,0:T(8,128)(2,1)S(1)}, u32[]{:S(2)}, u32[]{:S(2)}) async-start(bf16[16,8,2048]{2,1,0:T(8,128)(2,1)} %fusion.3), calls=%async_computation.2 | async-start | bytes 1048576 | tf_op jit(solution)/shard_map/all_to_all | solution.py:37
  56.9 1.7 copy-start.5
  58.6 1.2 copy-start.6
  58.6 1.9 copy-start.1
  59.9 0.6 copy-start.8
  73.1 21.4 %all-to-all-start.1 = ((bf16[16,2,8192]{2,1,0:T(2,128)(2,1)}), bf16[16,2,8192]{2,1,0:T(2,128)(2,1)}, u32[]{:S(2)}, u32[]{:S(2)}) async-start(bf16[16,2,8192]{2,1,0:T(2,128)(2,1)} %reshape.117), calls=%async_computation.1 | async-start | bytes 1048576 | tf_op jit(solution)/shard_map/all_to_all | solution.py:42
  78.5 1.4 copy-start.3
  78.5 1.4 copy-start.7
  78.5 1.4 copy-start.9
  94.5 20.4 %all-to-all-start.3 = ((bf16[16,2,8192]{2,1,0:T(2,128)(2,1)}), bf16[16,2,8192]{2,1,0:T(2,128)(2,1)S(1)}, u32[]{:S(2)}, u32[]{:S(2)}) async-start(bf16[16,2,8192]{2,1,0:T(2,128)(2,1)} %reshape.119), calls=%async_computation.3 | async-start | bytes 1048576 | tf_op jit(solution)/shard_map/all_to_all | solution.py:42
  98.7 79.4 %all-reduce.5.cloned.1.call-start = ((), (), s32[]{:S(2)}) async-start(), calls=%async_computation.6 | async-start | bytes 262144
  116.6 85.4 %reduce-scatter.4.cloned.1.call-start = ((), (), s32[]{:S(2)}) async-start(), calls=%async_computation.5 | async-start | bytes 1671168
Sparse Core Ops, SparseCore 0:
  116.7 61.4 all-reduce.4
Sparse Core Ops, SparseCore 1:
  127.3 74.7 reduce-scatter.3
where the time goes:
time: 212 us; the launch traced here: 211 us
  waiting for transfers between devices  96.5 us (46%)
  blocking collectives  33.9 us (16%)
  local copies, waits for them, and re-layouts  24.9 us (12%)
  starting transfers between devices  17.9 us (8%)
  between operations  16.4 us (8%)
  other arithmetic  10.9 us (5%)
  matrix products  10.8 us (5%)
    unnamed x4, waiting for transfers between devices  71.5 us
    all_gather x2, blocking collectives, dispatch(): gathered = lax.all_gather(rows, 'tensor', axis=0, tiled=True)  33.9 us
    unnamed x37, local copies, waits for them, and re-layouts  22.3 us
    all_to_all x2, waiting for transfers between devices, gather_back(): lax.all_to_all(partial_slots, 'expert', split_axis=1, concat_axis=0, tile...  20.4 us
    all_to_all x2, starting transfers between devices, gather_back(): lax.all_to_all(partial_slots, 'expert', split_axis=1, concat_axis=0, tile...  9.67 us
    unnamed x2, other arithmetic  9.28 us
    all_to_all x2, starting transfers between devices, dispatch(): lax.all_to_all(fill_slots(gathered, gain), 'expert', split_axis=0, concat...  8.11 us
    all_to_all x2, waiting for transfers between devices, dispatch(): lax.all_to_all(fill_slots(gathered, gain), 'expert', split_axis=0, concat...  4.6 us
  transfers between devices with their start and end apart: 6, of which 6 were waited for; matrix products, arithmetic and copies ran while one was open for 18% of the time, Pallas kernels for 0%

commit v1 on v0

v1 whole, which is shorter than its diff:
```python
import functools

import jax
import jax.numpy as jnp
from jax import lax
from jax.experimental import pallas as pl
from jax.experimental.pallas import tpu as pltpu
from jax.sharding import PartitionSpec as P

MESH = pl.DeviceIdType.MESH
F32 = jnp.float32
BF16 = jnp.bfloat16
SUB = 4


def dot(left, right):
    return lax.dot_general(left, right, (((1,), (0,)), ((), ())), preferred_element_type=F32)


def dot_t(left, right):
    return lax.dot_general(left, right, (((1,), (1,)), ((), ())), preferred_element_type=F32)


def kernel(
    n_z,
    n_e,
    tok_ref,
    cot_ref,
    routes_ref,
    pos_ref,
    cw_ref,
    gw_hbm,
    uw_hbm,
    dw_hbm,
    lo_ref,
    gt_ref,
    gd_ref,
    gw,
    uw,
    dw,
    xin,
    group,
    dsend,
    rows,
    gate_s,
    up_s,
    part,
    rs_far,
    rs_sum,
    rs_near,
    ysend,
    yret,
    csend,
    fin,
    term,
    zin,
    zout,
    w_sem,
    sx_sem,
    rx_sem,
    sd_sem,
    rd_sem,
    sg_sem,
    rg_sem,
    sr_sem,
    rr_sem,
    sy_sem,
    ry_sem,
    sc_sem,
    rc_sem,
    sz_sem,
    rz_sem,
):
    n_x, _, _, cap, q_cols = rows.shape[1:]
    tokens_here = tok_ref.shape[0]
    group_size = routes_ref.shape[0]
    n_slots = n_e * cap
    half_e = n_e // 2
    half_z = n_z // 2
    hidden = gate_s.shape[1]
    x = lax.axis_index("tensor")
    e = lax.axis_index("expert")
    z = lax.axis_index("dp")

    def x_at(d):
        return lax.rem(x + d + n_x, n_x)

    def e_at(d):
        return lax.rem(e + d + n_e, n_e)

    def z_at(d):
        return lax.rem(z + d + 2 * n_z, n_z)

    started = []

    def send(src, dst, send_sem, recv_sem, device):
        copy = pltpu.make_async_remote_copy(
            src_ref=src,
            dst_ref=dst,
            send_sem=send_sem,
            recv_sem=recv_sem,
            device_id=device,
            device_id_type=MESH,
        )
        copy.start()
        started.append(copy)

    def arrive(dst, send_sem, recv_sem, device):
        pltpu.make_async_remote_copy(
            src_ref=dst,
            dst_ref=dst,
            send_sem=send_sem,
            recv_sem=recv_sem,
            device_id=device,
            device_id_type=MESH,
        ).wait_recv()

    loads = []
    for i, (src, dst) in enumerate(((gw_hbm, gw), (uw_hbm, uw), (dw_hbm, dw))):
        load = pltpu.make_async_copy(src, dst, w_sem.at[i])
        load.start()
        loads.append(load)

    barrier = pltpu.get_barrier_semaphore()
    for d in range(1, n_x):
        pl.semaphore_signal(barrier, inc=1, device_id={"tensor": x_at(d)}, device_id_type=MESH)
    for d in range(1, n_e):
        pl.semaphore_signal(barrier, inc=1, device_id={"expert": e_at(d)}, device_id_type=MESH)
    for d in (1, -1):
        pl.semaphore_signal(barrier, inc=1, device_id={"dp": z_at(d)}, device_id_type=MESH)
    pl.semaphore_wait(barrier, n_x - 1 + n_e - 1 + 2)

    sources = (tok_ref, cot_ref)

    def quarter_of(a, q):
        return sources[a].at[:, pl.ds(pl.multiple_of(q * q_cols, q_cols), q_cols)]

    for a in range(2):
        for d in range(1, n_x):
            q = x_at(d)
            send(
                quarter_of(a, q),
                xin.at[a, x],
                sx_sem.at[a, d],
                rx_sem.at[a, d],
                {"tensor": q},
            )
    for a in range(2):
        xin[a, x] = quarter_of(a, x)[...]

    slot_ids = routes_ref[...] * cap + pos_ref[...]
    gains = cw_ref[...]
    lanes = lax.broadcasted_iota(jnp.int32, (group_size, n_slots), 1)
    placed = jnp.zeros((group_size, n_slots), F32)
    weighted = jnp.zeros((group_size, n_slots), F32)
    for k in range(slot_ids.shape[1]):
        match = lanes == slot_ids[:, k : k + 1]
        placed = placed + jnp.where(match, 1.0, 0.0)
        weighted = weighted + jnp.where(match, gains[:, k : k + 1], 0.0)

    def pieces(table):
        high = table.astype(BF16)
        return high, (table - high.astype(F32)).astype(BF16)

    placed_in = placed.T.astype(BF16)
    weighted_in = pieces(weighted.T)
    placed_back = placed.astype(BF16)
    weighted_back = pieces(weighted)

    def dispatch(a):
        for d in range(1, n_x):
            src = x_at(-d)
            arrive(xin.at[a, src], sx_sem.at[a, d], rx_sem.at[a, d], {"tensor": src})
        for j in range(n_x):
            group[pl.ds(j * tokens_here, tokens_here), :] = xin[a, j].astype(F32)
        here = group[...].astype(BF16)
        if a == 0:
            slots = dot(placed_in, here)
        else:
            slots = dot(weighted_in[0], here) + dot(weighted_in[1], here)
        dsend[a] = slots.reshape(n_e, cap, q_cols).astype(BF16).reshape(2, half_e, cap, q_cols)
        for d in range(1, n_e):
            to = e_at(d)
            send(
                dsend.at[a, to // half_e, lax.rem(to, half_e)],
                rows.at[a, x, e // half_e, lax.rem(e, half_e)],
                sd_sem.at[a, d],
                rd_sem.at[a, d],
                {"expert": to},
            )
        rows[a, x, e // half_e, lax.rem(e, half_e)] = dsend[a, e // half_e, lax.rem(e, half_e)]

    def dispatch_wait(a):
        for d in range(1, n_e):
            src = e_at(-d)
            arrive(
                rows.at[a, x, src // half_e, lax.rem(src, half_e)],
                sd_sem.at[a, d],
                rd_sem.at[a, d],
                {"expert": src},
            )

    right, left = x_at(1), x_at(-1)
    far = x_at(2)

    def gather_start(a):
        for h in range(2):
            send(rows.at[a, x, h], rows.at[a, x, h], sg_sem.at[a, 0, h], rg_sem.at[a, 0, h], {"tensor": right})
            g = 1 - h
            send(rows.at[a, x, g], rows.at[a, x, g], sg_sem.at[a, 1, g], rg_sem.at[a, 1, g], {"tensor": left})

    def gather_relay(a):
        arrive(rows.at[a, left, 0], sg_sem.at[a, 0, 0], rg_sem.at[a, 0, 0], {"tensor": left})
        send(rows.at[a, left, 0], rows.at[a, left, 0], sg_sem.at[a, 2, 0], rg_sem.at[a, 2, 0], {"tensor": right})
        arrive(rows.at[a, right, 1], sg_sem.at[a, 1, 1], rg_sem.at[a, 1, 1], {"tensor": right})
        send(rows.at[a, right, 1], rows.at[a, right, 1], sg_sem.at[a, 2, 1], rg_sem.at[a, 2, 1], {"tensor": left})

    def gather_near(a):
        arrive(rows.at[a, left, 1], sg_sem.at[a, 0, 1], rg_sem.at[a, 0, 1], {"tensor": left})
        arrive(rows.at[a, right, 0], sg_sem.at[a, 1, 0], rg_sem.at[a, 1, 0], {"tensor": right})

    def gather_far(a):
        arrive(rows.at[a, far, 0], sg_sem.at[a, 2, 0], rg_sem.at[a, 2, 0], {"tensor": left})
        arrive(rows.at[a, far, 1], sg_sem.at[a, 2, 1], rg_sem.at[a, 2, 1], {"tensor": right})

    def row_block(a, q):
        return rows[a, q].reshape(n_slots, q_cols)

    def put_part(b, q, value):
        part[b, q] = value.reshape(n_e, cap, q_cols).astype(BF16).reshape(2, half_e, cap, q_cols)

    def reduce_far(b):
        send(part.at[b, far, 0], rs_far.at[b, 0], sr_sem.at[b, 0], rr_sem.at[b, 0], {"tensor": right})
        send(part.at[b, far, 1], rs_far.at[b, 1], sr_sem.at[b, 1], rr_sem.at[b, 1], {"tensor": left})

    def reduce_near(b):
        send(part.at[b, right, 1], rs_near.at[b, 0, 1], sr_sem.at[b, 2], rr_sem.at[b, 2], {"tensor": right})
        send(part.at[b, left, 0], rs_near.at[b, 1, 0], sr_sem.at[b, 3], rr_sem.at[b, 3], {"tensor": left})

    def reduce_relay(b):
        arrive(rs_far.at[b, 0], sr_sem.at[b, 0], rr_sem.at[b, 0], {"tensor": left})
        rs_sum[b, 0] = (rs_far[b, 0].astype(F32) + part[b, right, 0].astype(F32)).astype(BF16)
        send(rs_sum.at[b, 0], rs_near.at[b, 0, 0], sr_sem.at[b, 4], rr_sem.at[b, 4], {"tensor": right})
        arrive(rs_far.at[b, 1], sr_sem.at[b, 1], rr_sem.at[b, 1], {"tensor": right})
        rs_sum[b, 1] = (rs_far[b, 1].astype(F32) + part[b, left, 1].astype(F32)).astype(BF16)
        send(rs_sum.at[b, 1], rs_near.at[b, 1, 1], sr_sem.at[b, 5], rr_sem.at[b, 5], {"tensor": left})

    def reduce_end(b):
        arrive(rs_near.at[b, 0, 1], sr_sem.at[b, 2], rr_sem.at[b, 2], {"tensor": left})
        arrive(rs_near.at[b, 1, 0], sr_sem.at[b, 3], rr_sem.at[b, 3], {"tensor": right})
        arrive(rs_near.at[b, 0, 0], sr_sem.at[b, 4], rr_sem.at[b, 4], {"tensor": left})
        arrive(rs_near.at[b, 1, 1], sr_sem.at[b, 5], rr_sem.at[b, 5], {"tensor": right})
        total = part[b, x].astype(F32) + rs_near[b, 0].astype(F32) + rs_near[b, 1].astype(F32)
        ysend[b] = total.astype(BF16)
        for d in range(1, n_e):
            to = e_at(d)
            send(
                ysend.at[b, to // half_e, lax.rem(to, half_e)],
                yret.at[b, e // half_e, lax.rem(e, half_e)],
                sy_sem.at[b, d],
                ry_sem.at[b, d],
                {"expert": to},
            )
        yret[b, e // half_e, lax.rem(e, half_e)] = ysend[b, e // half_e, lax.rem(e, half_e)]

    def combine(b):
        for d in range(1, n_e):
            src = e_at(-d)
            arrive(
                yret.at[b, src // half_e, lax.rem(src, half_e)],
                sy_sem.at[b, d],
                ry_sem.at[b, d],
                {"expert": src},
            )
        slots = yret[b].reshape(n_slots, q_cols)
        if b == 0:
            mixed = dot(weighted_back[0], slots) + dot(weighted_back[1], slots)
        else:
            mixed = dot(placed_back, slots)
        group[...] = mixed
        for j in range(n_x):
            csend[b, j] = group[pl.ds(j * tokens_here, tokens_here), :].astype(BF16)
        for d in range(1, n_x):
            to = x_at(d)
            send(csend.at[b, to], fin.at[b, x], sc_sem.at[b, d], rc_sem.at[b, d], {"tensor": to})
        fin[b, x] = csend[b, x]

    def finish(b, out_ref):
        for d in range(1, n_x):
            src = x_at(-d)
            arrive(fin.at[b, src], sc_sem.at[b, d], rc_sem.at[b, d], {"tensor": src})
        for j in range(n_x):
            out_ref[:, pl.ds(j * q_cols, q_cols)] = fin[b, j]

    z_up, z_down = z_at(1), z_at(-1)

    def z_send(way, s, i):
        send(
            zout.at[way, s, i],
            zin.at[way, s, i],
            sz_sem.at[way, s, i],
            rz_sem.at[way, s, i],
            {"dp": z_up if way == 0 else z_down},
        )

    def z_arrive(way, s, i):
        arrive(
            zin.at[way, s, i],
            sz_sem.at[way, s, i],
            rz_sem.at[way, s, i],
            {"dp": z_down if way == 0 else z_up},
        )
        return zin[way, s, i].astype(F32)

    def z_step(s):
        targets = (z_at(half_z - s), z_at(s - half_z))
        for j in range(SUB if s > 0 else SUB // 2):
            early = j < SUB // 2
            for way in range(2):
                i = j if way == 0 else SUB - 1 - j
                value = term[targets[way], i]
                if s > 1 or (s == 1 and early):
                    value = value + z_arrive(way, s - 1, i)
                zout[way, s, i] = value.astype(BF16)
                z_send(way, s, i)

    def z_finish():
        for i in range(SUB):
            total = term[z, i] + z_arrive(0, half_z - 1, i) + z_arrive(1, half_z - 1, i)
            term[z, i] = total * (1.0 / n_z)
        whole = term[z].reshape(hidden, term.shape[3])
        gd_ref[...] = whole.T.astype(BF16)

    dispatch(0)
    dispatch(1)
    dispatch_wait(0)
    gather_start(0)
    loads[0].wait()
    loads[1].wait()
    block = row_block(0, x)
    gate_s[...] = dot(block, gw[x])
    up_s[...] = dot(block, uw[x])
    dispatch_wait(1)
    gather_start(1)
    gather_relay(0)
    gather_near(0)
    for q in (left, right):
        block = row_block(0, q)
        gate_s[...] += dot(block, gw[q])
        up_s[...] += dot(block, uw[q])
    gather_far(0)
    block = row_block(0, far)
    gate = gate_s[...] + dot(block, gw[far])
    up = up_s[...] + dot(block, uw[far])
    squash = 1.0 / (1.0 + jnp.exp(-gate))
    swish = gate * squash
    act = swish * up
    gate_s[...] = up * squash * (1.0 + gate * (1.0 - squash))
    up_s[...] = swish
    act_b = act.astype(BF16)
    act_t = act.T.astype(BF16)
    loads[2].wait()
    gather_relay(1)
    put_part(0, far, dot_t(act_b, dw[far]))
    reduce_far(0)
    for q in (right, left):
        put_part(0, q, dot_t(act_b, dw[q]))
    reduce_near(0)
    put_part(0, x, dot_t(act_b, dw[x]))
    gather_near(1)
    gather_far(1)
    chunk_cols = term.shape[3]
    per_quarter = q_cols // chunk_cols
    for q in range(n_x):
        block = dot(act_t, row_block(1, q))
        for c in range(per_quarter):
            piece = block[:, c * chunk_cols : (c + 1) * chunk_cols]
            term[q * per_quarter + c] = piece.reshape(SUB, hidden // SUB, chunk_cols)
    z_step(0)
    reduce_relay(0)
    grad = None
    for q in range(n_x):
        piece = dot(row_block(1, q), dw[q])
        grad = piece if grad is None else grad + piece
    gate_back = (grad * gate_s[...]).astype(BF16)
    up_back = (grad * up_s[...]).astype(BF16)
    z_step(1)

    def input_part(q):
        put_part(1, q, dot_t(gate_back, gw[q]) + dot_t(up_back, uw[q]))

    input_part(far)
    reduce_far(1)
    input_part(right)
    input_part(left)
    reduce_near(1)
    reduce_end(0)
    z_step(2)
    input_part(x)
    reduce_relay(1)
    z_step(3)
    reduce_end(1)
    combine(0)
    z_step(4)
    z_step(5)
    combine(1)
    finish(0, lo_ref)
    z_step(6)
    finish(1, gt_ref)
    z_step(7)
    z_finish()
    for copy in started:
        copy.wait_send()


def shards(
    tokens, routes, positions, combine_weights, cotangent, gate_weight, up_weight, down_weight
):
    n_z, n_e, n_x = lax.axis_size("dp"), lax.axis_size("expert"), lax.axis_size("tensor")
    tokens_here, width = tokens.shape
    group_size = routes.shape[0]
    cap = group_size // 2
    hidden = gate_weight.shape[2]
    q_cols = width // n_x
    n_slots = n_e * cap
    half_e, half_z = n_e // 2, n_z // 2
    z_rows = width // n_z
    vmem = pl.BlockSpec(memory_space=pltpu.VMEM)
    hbm = pl.BlockSpec(memory_space=pl.ANY)
    dma = pltpu.SemaphoreType.DMA
    weights = [
        w.reshape(n_x, q_cols, hidden) for w in (gate_weight, up_weight, down_weight)
    ]
    quarter = (half_e, cap, q_cols)
    return pl.pallas_call(
        functools.partial(kernel, n_z, n_e),
        out_shape=(
            jax.ShapeDtypeStruct((tokens_here, width), BF16),
            jax.ShapeDtypeStruct((tokens_here, width), BF16),
            jax.ShapeDtypeStruct((z_rows, hidden), BF16),
        ),
        in_specs=[vmem] * 5 + [hbm] * 3,
        out_specs=(vmem, vmem, vmem),
        scratch_shapes=[pltpu.VMEM((n_x, q_cols, hidden), BF16)] * 3
        + [
            pltpu.VMEM((2, n_x, tokens_here, q_cols), BF16),
            pltpu.VMEM((group_size, q_cols), F32),
            pltpu.VMEM((2, 2) + quarter, BF16),
            pltpu.VMEM((2, n_x, 2) + quarter, BF16),
            pltpu.VMEM((n_slots, hidden), F32),
            pltpu.VMEM((n_slots, hidden), F32),
            pltpu.VMEM((2, n_x, 2) + quarter, BF16),
            pltpu.VMEM((2, 2) + quarter, BF16),
            pltpu.VMEM((2, 2) + quarter, BF16),
            pltpu.VMEM((2, 2, 2) + quarter, BF16),
            pltpu.VMEM((2, 2) + quarter, BF16),
            pltpu.VMEM((2, 2) + quarter, BF16),
            pltpu.VMEM((2, n_x, tokens_here, q_cols), BF16),
            pltpu.VMEM((2, n_x, tokens_here, q_cols), BF16),
            pltpu.VMEM((n_z, SUB, hidden // SUB, z_rows), F32),
            pltpu.VMEM((2, half_z, SUB, hidden // SUB, z_rows), BF16),
            pltpu.VMEM((2, half_z, SUB, hidden // SUB, z_rows), BF16),
            dma((3,)),
            dma((2, n_x)),
            dma((2, n_x)),
            dma((2, n_e)),
            dma((2, n_e)),
            dma((2, 3, 2)),
            dma((2, 3, 2)),
            dma((2, 6)),
            dma((2, 6)),
            dma((2, n_e)),
            dma((2, n_e)),
            dma((2, n_x)),
            dma((2, n_x)),
            dma((2, half_z, SUB)),
            dma((2, half_z, SUB)),
        ],
        compiler_params=pltpu.CompilerParams(
            collective_id=0, has_side_effects=True, vmem_limit_bytes=56 * 1024 * 1024
        ),
    )(tokens, cotangent, routes, positions, combine_weights, *weights)


def body(*arrays):
    layer_out, grad_tokens, grad_down = shards(*arrays)
    return layer_out, grad_tokens, grad_down[None]


def solution(mesh):
    return jax.shard_map(
        body,
        mesh=mesh,
        in_specs=(
            P(("dp", "expert", "tensor"), None),
            P(("dp", "expert"), None),
            P(("dp", "expert"), None),
            P(("dp", "expert"), None),
            P(("dp", "expert", "tensor"), None),
            P("expert", None, "tensor"),
            P("expert", None, "tensor"),
            P("expert", None, "tensor"),
        ),
        out_specs=(
            P(("dp", "expert", "tensor"), None),
            P(("dp", "expert", "tensor"), None),
            P("expert", "dp", "tensor"),
        ),
        check_vma=False,
    )
```

time: 212 us -> 92.9 us (0.44)
  the two profiles are of different devices: /device:TPU:6 before, /device:TPU:1 now
where the time goes in v1:
time: 92.9 us; the launch traced here: 91.8 us
  Pallas kernels  77 us (83%)
  local copies, waits for them, and re-layouts  14.2 us (15%)
    pallas_call x1, Pallas kernels, shards(): pl.pallas_call(functools.partial(kernel, n_z, n_e), out_shape=(jax.ShapeD...  77 us
    unnamed x13, local copies, waits for them, and re-layouts  14.2 us

profile of v1, /device:TPU:1, one launch (start us, length us, event | category | flops | bytes accessed | tf_op | source)
XLA Modules:
  0.0 91.8 jit_solution(6740742364122816415)
XLA Ops:
  0.6 0.0 copy-start
  0.6 1.5 %copy.14.routes_ref = s32[16,6]{1,0:T(8,128)} copy(s32[16,6]{0,1:T(8,128)} %param.9) | data formatting | bytes 768 | tf_op args[1]
  2.1 1.4 %copy.15.pos_ref = s32[16,6]{1,0:T(8,128)} copy(s32[16,6]{0,1:T(8,128)} %param.10) | data formatting | bytes 768 | tf_op args[2]
  3.5 1.4 %copy.16.cw_ref = f32[16,6]{1,0:T(8,128)} copy(f32[16,6]{0,1:T(8,128)} %param.11) | data formatting | bytes 768 | tf_op args[3]
  4.8 2.6 %copy.11 = bf16[1,2048,352]{2,1,0:T(8,128)(2,1)} copy(bf16[1,2048,352]{1,2,0:T(8,128)(2,1)} %param.13) | data formatting | bytes 2883584 | tf_op args[5]
  7.4 0.0 copy-start.1
  7.4 0.0 copy-done
  7.4 1.6 %copy.12 = bf16[1,2048,352]{2,1,0:T(8,128)(2,1)} copy(bf16[1,2048,352]{1,2,0:T(8,128)(2,1)S(1)} %copy-done) | data formatting | bytes 2883584 | tf_op args[6]
  9.0 0.0 copy-done.1
  9.0 1.6 %copy.13 = bf16[1,2048,352]{2,1,0:T(8,128)(2,1)} copy(bf16[1,2048,352]{1,2,0:T(8,128)(2,1)S(1)} %copy-done.1) | data formatting | bytes 2883584 | tf_op args[7]
  10.5 77.0 %shard_map.103 = (bf16[4,2048]{1,0:T(4,128)(2,1)}, bf16[4,2048]{1,0:T(4,128)(2,1)}, bf16[128,352]{1,0:T(8,128)(2,1)}) custom-call(bf16[4,2048]{1,0:T(4,128)(2,1)} %tok_ref.1, bf16[4,2048]{1,0:T(4,128)(2,1)} %cot_ref.1, s32[16,6]{1,0:T(8,128)} %copy.14.routes_ref, s32[16,6]{1,0:T(8,128)} %copy.15.pos_ref, f32[16,6]{1,0:T(8,128)} %copy.16.cw_ref, ...), custom_call_target="tpu_custom_call" | custom-call | tf_op jit(solution)/shard_map/pallas_call | solution.py:435
  87.5 1.6 %copy.17 = bf16[1,128,352]{1,2,0:T(8,128)(2,1)} copy(bf16[1,128,352]{2,1,0:T(8,128)(2,1)} %bitcast.7) | data formatting | bytes 180224
  89.2 1.3 %copy.20 = bf16[4,2048]{1,0:T(4,128)(2,1)} copy(bf16[4,2048]{1,0:T(4,128)(2,1)} %get-tuple-element.15) | data formatting | bytes 32768
  90.5 1.3 %copy.21 = bf16[4,2048]{1,0:T(4,128)(2,1)} copy(bf16[4,2048]{1,0:T(4,128)(2,1)} %get-tuple-element.16) | data formatting | bytes 32768
Async XLA Ops:
  0.6 6.8 %copy-start = (bf16[1,2048,352]{1,2,0:T(8,128)(2,1)S(1)}, bf16[1,2048,352]{1,2,0:T(8,128)(2,1)}, u32[]{:S(2)}) copy-start(bf16[1,2048,352]{1,2,0:T(8,128)(2,1)} %param.14) | copy-start | bytes 4325380
  7.4 1.6 %copy-start.1 = (bf16[1,2048,352]{1,2,0:T(8,128)(2,1)S(1)}, bf16[1,2048,352]{1,2,0:T(8,128)(2,1)}, u32[]{:S(2)}) copy-start(bf16[1,2048,352]{1,2,0:T(8,128)(2,1)} %param.15) | copy-start | bytes 4325380

commit v2 on v1

--- a/solution.py
+++ b/solution.py
@@ -73,7 +73,7 @@
 ):
     n_x, _, _, cap, q_cols = rows.shape[1:]
     tokens_here = tok_ref.shape[0]
-    group_size = routes_ref.shape[0]
+    group_size = routes_ref.shape[1]
     n_slots = n_e * cap
     half_e = n_e // 2
     half_z = n_z // 2
@@ -150,22 +150,22 @@
 
     slot_ids = routes_ref[...] * cap + pos_ref[...]
     gains = cw_ref[...]
-    lanes = lax.broadcasted_iota(jnp.int32, (group_size, n_slots), 1)
-    placed = jnp.zeros((group_size, n_slots), F32)
-    weighted = jnp.zeros((group_size, n_slots), F32)
-    for k in range(slot_ids.shape[1]):
-        match = lanes == slot_ids[:, k : k + 1]
+    numbers = lax.broadcasted_iota(jnp.int32, (n_slots, group_size), 0)
+    placed = jnp.zeros((n_slots, group_size), F32)
+    weighted = jnp.zeros((n_slots, group_size), F32)
+    for k in range(slot_ids.shape[0]):
+        match = numbers == slot_ids[k : k + 1, :]
         placed = placed + jnp.where(match, 1.0, 0.0)
-        weighted = weighted + jnp.where(match, gains[:, k : k + 1], 0.0)
+        weighted = weighted + jnp.where(match, gains[k : k + 1, :], 0.0)
 
     def pieces(table):
         high = table.astype(BF16)
         return high, (table - high.astype(F32)).astype(BF16)
 
-    placed_in = placed.T.astype(BF16)
-    weighted_in = pieces(weighted.T)
-    placed_back = placed.astype(BF16)
-    weighted_back = pieces(weighted)
+    placed_in = placed.astype(BF16)
+    weighted_in = pieces(weighted)
+    placed_back = placed.T.astype(BF16)
+    weighted_back = pieces(weighted.T)
 
     def dispatch(a):
         for d in range(1, n_x):
@@ -223,6 +223,9 @@
         arrive(rows.at[a, far, 0], sg_sem.at[a, 2, 0], rg_sem.at[a, 2, 0], {"tensor": left})
         arrive(rows.at[a, far, 1], sg_sem.at[a, 2, 1], rg_sem.at[a, 2, 1], {"tensor": right})
 
+    def weight(ref, q):
+        return ref[:, pl.ds(pl.multiple_of(q * q_cols, q_cols), q_cols)]
+
     def row_block(a, q):
         return rows[a, q].reshape(n_slots, q_cols)
 
@@ -327,9 +330,8 @@
     def z_finish():
         for i in range(SUB):
             total = term[z, i] + z_arrive(0, half_z - 1, i) + z_arrive(1, half_z - 1, i)
-            term[z, i] = total * (1.0 / n_z)
-        whole = term[z].reshape(hidden, term.shape[3])
-        gd_ref[...] = whole.T.astype(BF16)
+            rows_here = hidden // SUB
+            gd_ref[pl.ds(i * rows_here, rows_here), :] = (total * (1.0 / n_z)).astype(BF16)
 
     dispatch(0)
     dispatch(1)
@@ -338,20 +340,20 @@
     loads[0].wait()
     loads[1].wait()
     block = row_block(0, x)
-    gate_s[...] = dot(block, gw[x])
-    up_s[...] = dot(block, uw[x])
+    gate_s[...] = dot_t(block, weight(gw, x))
+    up_s[...] = dot_t(block, weight(uw, x))
     dispatch_wait(1)
     gather_start(1)
     gather_relay(0)
     gather_near(0)
     for q in (left, right):
         block = row_block(0, q)
-        gate_s[...] += dot(block, gw[q])
-        up_s[...] += dot(block, uw[q])
+        gate_s[...] += dot_t(block, weight(gw, q))
+        up_s[...] += dot_t(block, weight(uw, q))
     gather_far(0)
     block = row_block(0, far)
-    gate = gate_s[...] + dot(block, gw[far])
-    up = up_s[...] + dot(block, uw[far])
+    gate = gate_s[...] + dot_t(block, weight(gw, far))
+    up = up_s[...] + dot_t(block, weight(uw, far))
     squash = 1.0 / (1.0 + jnp.exp(-gate))
     swish = gate * squash
     act = swish * up
@@ -361,12 +363,12 @@
     act_t = act.T.astype(BF16)
     loads[2].wait()
     gather_relay(1)
-    put_part(0, far, dot_t(act_b, dw[far]))
+    put_part(0, far, dot(act_b, weight(dw, far)))
     reduce_far(0)
     for q in (right, left):
-        put_part(0, q, dot_t(act_b, dw[q]))
+        put_part(0, q, dot(act_b, weight(dw, q)))
     reduce_near(0)
-    put_part(0, x, dot_t(act_b, dw[x]))
+    put_part(0, x, dot(act_b, weight(dw, x)))
     gather_near(1)
     gather_far(1)
     chunk_cols = term.shape[3]
@@ -380,14 +382,14 @@
     reduce_relay(0)
     grad = None
     for q in range(n_x):
-        piece = dot(row_block(1, q), dw[q])
+        piece = dot_t(row_block(1, q), weight(dw, q))
         grad = piece if grad is None else grad + piece
     gate_back = (grad * gate_s[...]).astype(BF16)
     up_back = (grad * up_s[...]).astype(BF16)
     z_step(1)
 
     def input_part(q):
-        put_part(1, q, dot_t(gate_back, gw[q]) + dot_t(up_back, uw[q]))
+        put_part(1, q, dot(gate_back, weight(gw, q)) + dot(up_back, weight(uw, q)))
 
     input_part(far)
     reduce_far(1)
@@ -428,20 +430,19 @@
     vmem = pl.BlockSpec(memory_space=pltpu.VMEM)
     hbm = pl.BlockSpec(memory_space=pl.ANY)
     dma = pltpu.SemaphoreType.DMA
-    weights = [
-        w.reshape(n_x, q_cols, hidden) for w in (gate_weight, up_weight, down_weight)
-    ]
+    weights = [jnp.swapaxes(w[0], 0, 1) for w in (gate_weight, up_weight, down_weight)]
+    plans = [v.T for v in (routes, positions, combine_weights)]
     quarter = (half_e, cap, q_cols)
     return pl.pallas_call(
         functools.partial(kernel, n_z, n_e),
         out_shape=(
             jax.ShapeDtypeStruct((tokens_here, width), BF16),
             jax.ShapeDtypeStruct((tokens_here, width), BF16),
-            jax.ShapeDtypeStruct((z_rows, hidden), BF16),
+            jax.ShapeDtypeStruct((hidden, z_rows), BF16),
         ),
         in_specs=[vmem] * 5 + [hbm] * 3,
         out_specs=(vmem, vmem, vmem),
-        scratch_shapes=[pltpu.VMEM((n_x, q_cols, hidden), BF16)] * 3
+        scratch_shapes=[pltpu.VMEM((hidden, width), BF16)] * 3
         + [
             pltpu.VMEM((2, n_x, tokens_here, q_cols), BF16),
             pltpu.VMEM((group_size, q_cols), F32),
@@ -479,12 +480,24 @@
         compiler_params=pltpu.CompilerParams(
             collective_id=0, has_side_effects=True, vmem_limit_bytes=56 * 1024 * 1024
         ),
-    )(tokens, cotangent, routes, positions, combine_weights, *weights)
+    )(tokens, cotangent, *plans, *weights)
+
+
+def place(*refs):
+    half = len(refs) // 2
+    for source, target in zip(refs[:half], refs[half:]):
+        target[...] = source[...]
 
 
 def body(*arrays):
-    layer_out, grad_tokens, grad_down = shards(*arrays)
-    return layer_out, grad_tokens, grad_down[None]
+    results = shards(*arrays)
+    layer_out, grad_tokens, grad_down = pl.pallas_call(
+        place,
+        out_shape=tuple(jax.ShapeDtypeStruct(r.shape, r.dtype) for r in results),
+        in_specs=[pl.BlockSpec(memory_space=pltpu.VMEM)] * 3,
+        out_specs=(pl.BlockSpec(memory_space=pltpu.VMEM),) * 3,
+    )(*results)
+    return layer_out, grad_tokens, jnp.swapaxes(grad_down, 0, 1)[None]
 
 
 def solution(mesh):

time: 92.9 us -> 80 us (0.86)
  local copies, waits for them, and re-layouts: 14.2 us -> 0 us
  Pallas kernels: 77 us -> 78.5 us
    unnamed x13 -> x0, local copies, waits for them, and re-layouts: 14.2 us -> none
    pallas_call x0 -> x1, Pallas kernels: none -> 1.58 us  [body(): pl.pallas_call(place, out_shape=tuple((jax.ShapeDtypeStruct(r.shape, r.dt...]
where the time goes in v2:
time: 80 us; the launch traced here: 79.1 us
  Pallas kernels  78.5 us (98%)
    pallas_call x1, Pallas kernels, shards(): pl.pallas_call(functools.partial(kernel, n_z, n_e), out_shape=(jax.ShapeD...  76.9 us

profile of v2, /device:TPU:1, one launch (start us, length us, event | category | flops | bytes accessed | tf_op | source)
XLA Modules:
  0.0 79.1 jit_solution(12571942955900157834)
XLA Ops:
  0.6 76.9 %shard_map.103 = (bf16[4,2048]{1,0:T(4,128)(2,1)}, bf16[4,2048]{1,0:T(4,128)(2,1)}, bf16[352,128]{1,0:T(8,128)(2,1)}) custom-call(bf16[4,2048]{1,0:T(4,128)(2,1)} %tok_ref.1, bf16[4,2048]{1,0:T(4,128)(2,1)} %cot_ref.1, s32[6,16]{1,0:T(8,128)} %bitcast.18, s32[6,16]{1,0:T(8,128)} %bitcast.19, f32[6,16]{1,0:T(8,128)} %bitcast.20, bf16[352,2048]{1,0:T(8,128)(2,1)} %bitcast.15, ...), custom_call_target="tpu_custom_call" | custom-call | tf_op jit(solution)/shard_map/pallas_call | solution.py:436
  77.5 1.6 %shard_map.104 = (bf16[4,2048]{1,0:T(4,128)(2,1)}, bf16[4,2048]{1,0:T(4,128)(2,1)}, bf16[352,128]{1,0:T(8,128)(2,1)}) custom-call(bf16[4,2048]{1,0:T(4,128)(2,1)} %get-tuple-element.9.refs_0_, bf16[4,2048]{1,0:T(4,128)(2,1)} %get-tuple-element.10.refs_1_, bf16[352,128]{1,0:T(8,128)(2,1)} %get-tuple-element.11.refs_2_), custom_call_target="tpu_custom_call" | custom-call | tf_op jit(solution)/shard_map/pallas_call | solution.py:494

commit v3 on v2

--- a/solution.py
+++ b/solution.py
@@ -24,17 +24,22 @@
 def kernel(
     n_z,
     n_e,
+    tok_hbm,
+    cot_hbm,
+    routes_hbm,
+    pos_hbm,
+    cw_hbm,
+    gw_hbm,
+    uw_hbm,
+    dw_hbm,
+    lo_hbm,
+    gt_hbm,
+    gd_hbm,
     tok_ref,
     cot_ref,
     routes_ref,
     pos_ref,
     cw_ref,
-    gw_hbm,
-    uw_hbm,
-    dw_hbm,
-    lo_ref,
-    gt_ref,
-    gd_ref,
     gw,
     uw,
     dw,
@@ -51,10 +56,14 @@
     ysend,
     yret,
     csend,
-    fin,
+    acts,
+    pair,
     term,
     zin,
     zout,
+    gd_out,
+    in_sem,
+    out_sem,
     w_sem,
     sx_sem,
     rx_sem,
@@ -68,6 +77,10 @@
     ry_sem,
     sc_sem,
     rc_sem,
+    sa_sem,
+    ra_sem,
+    sp_sem,
+    rp_sem,
     sz_sem,
     rz_sem,
 ):
@@ -76,7 +89,8 @@
     group_size = routes_ref.shape[1]
     n_slots = n_e * cap
     half_e = n_e // 2
-    half_z = n_z // 2
+    n_pairs = n_z // 2
+    half_z = n_pairs // 2
     hidden = gate_s.shape[1]
     x = lax.axis_index("tensor")
     e = lax.axis_index("expert")
@@ -115,20 +129,38 @@
             device_id_type=MESH,
         ).wait_recv()
 
+    fetches = []
+    for i, (src, dst) in enumerate(
+        (
+            (routes_hbm, routes_ref),
+            (pos_hbm, pos_ref),
+            (cw_hbm, cw_ref),
+            (tok_hbm, tok_ref),
+            (cot_hbm, cot_ref),
+        )
+    ):
+        fetch = pltpu.make_async_copy(src, dst, in_sem.at[i])
+        fetch.start()
+        fetches.append(fetch)
+    barrier = pltpu.get_barrier_semaphore()
+    for d in range(1, n_x):
+        pl.semaphore_signal(barrier, inc=1, device_id={"tensor": x_at(d)}, device_id_type=MESH)
+    for d in range(1, n_e):
+        pl.semaphore_signal(barrier, inc=1, device_id={"expert": e_at(d)}, device_id_type=MESH)
+    z_side = lax.rem(z, 2)
+    partner = z + 1 - 2 * z_side
+    z_up, z_down = z_at(2), z_at(-2)
+    for to in (partner, z_up, z_down):
+        pl.semaphore_signal(barrier, inc=1, device_id={"dp": to}, device_id_type=MESH)
     loads = []
     for i, (src, dst) in enumerate(((gw_hbm, gw), (uw_hbm, uw), (dw_hbm, dw))):
         load = pltpu.make_async_copy(src, dst, w_sem.at[i])
         load.start()
         loads.append(load)
 
-    barrier = pltpu.get_barrier_semaphore()
-    for d in range(1, n_x):
-        pl.semaphore_signal(barrier, inc=1, device_id={"tensor": x_at(d)}, device_id_type=MESH)
-    for d in range(1, n_e):
-        pl.semaphore_signal(barrier, inc=1, device_id={"expert": e_at(d)}, device_id_type=MESH)
-    for d in (1, -1):
-        pl.semaphore_signal(barrier, inc=1, device_id={"dp": z_at(d)}, device_id_type=MESH)
-    pl.semaphore_wait(barrier, n_x - 1 + n_e - 1 + 2)
+    for fetch in fetches:
+        fetch.wait()
+    pl.semaphore_wait(barrier, n_x - 1 + n_e - 1 + 3)
 
     sources = (tok_ref, cot_ref)
 
@@ -203,11 +235,10 @@
     right, left = x_at(1), x_at(-1)
     far = x_at(2)
 
-    def gather_start(a):
-        for h in range(2):
-            send(rows.at[a, x, h], rows.at[a, x, h], sg_sem.at[a, 0, h], rg_sem.at[a, 0, h], {"tensor": right})
-            g = 1 - h
-            send(rows.at[a, x, g], rows.at[a, x, g], sg_sem.at[a, 1, g], rg_sem.at[a, 1, g], {"tensor": left})
+    def gather_start(a, h):
+        g = 1 - h
+        send(rows.at[a, x, h], rows.at[a, x, h], sg_sem.at[a, 0, h], rg_sem.at[a, 0, h], {"tensor": right})
+        send(rows.at[a, x, g], rows.at[a, x, g], sg_sem.at[a, 1, g], rg_sem.at[a, 1, g], {"tensor": left})
 
     def gather_relay(a):
         arrive(rows.at[a, left, 0], sg_sem.at[a, 0, 0], rg_sem.at[a, 0, 0], {"tensor": left})
@@ -265,6 +296,12 @@
                 {"expert": to},
             )
         yret[b, e // half_e, lax.rem(e, half_e)] = ysend[b, e // half_e, lax.rem(e, half_e)]
+
+    stores = []
+    results = (lo_hbm, gt_hbm)
+
+    def result_of(b, q):
+        return results[b].at[:, pl.ds(pl.multiple_of(q * q_cols, q_cols), q_cols)]
 
     def combine(b):
         for d in range(1, n_e):
@@ -285,17 +322,54 @@
             csend[b, j] = group[pl.ds(j * tokens_here, tokens_here), :].astype(BF16)
         for d in range(1, n_x):
             to = x_at(d)
-            send(csend.at[b, to], fin.at[b, x], sc_sem.at[b, d], rc_sem.at[b, d], {"tensor": to})
-        fin[b, x] = csend[b, x]
-
-    def finish(b, out_ref):
+            send(csend.at[b, to], result_of(b, x), sc_sem.at[b, d], rc_sem.at[b, d], {"tensor": to})
+        own = pltpu.make_async_copy(csend.at[b, x], result_of(b, x), out_sem.at[b])
+        own.start()
+        stores.append(own)
+
+    def finish(b):
         for d in range(1, n_x):
             src = x_at(-d)
-            arrive(fin.at[b, src], sc_sem.at[b, d], rc_sem.at[b, d], {"tensor": src})
-        for j in range(n_x):
-            out_ref[:, pl.ds(j * q_cols, q_cols)] = fin[b, j]
-
-    z_up, z_down = z_at(1), z_at(-1)
+            arrive(result_of(b, src), sc_sem.at[b, d], rc_sem.at[b, d], {"tensor": src})
+
+    chunk_cols = term.shape[3]
+    pair_chunks = q_cols // chunk_cols // 2
+
+    def act_send():
+        send(acts.at[0], acts.at[1], sa_sem.at[0], ra_sem.at[0], {"dp": partner})
+
+    def act_arrive():
+        arrive(acts.at[1], sa_sem.at[0], ra_sem.at[0], {"dp": partner})
+
+    def columns(q, m, side):
+        start = pl.multiple_of((2 * m + side) * chunk_cols, chunk_cols)
+        return rows.at[1, q, :, :, :, pl.ds(start, chunk_cols)]
+
+    def pair_send(q):
+        for m in range(pair_chunks):
+            send(
+                columns(q, m, 1 - z_side),
+                pair.at[q, m],
+                sp_sem.at[q, m],
+                rp_sem.at[q, m],
+                {"dp": partner},
+            )
+
+    def pair_arrive(q):
+        for m in range(pair_chunks):
+            arrive(pair.at[q, m], sp_sem.at[q, m], rp_sem.at[q, m], {"dp": partner})
+
+    place_z = z // 2
+
+    def pair_at(d):
+        return lax.rem(place_z + d + 2 * n_pairs, n_pairs)
+
+    def make_term(target):
+        q, m = target // pair_chunks, lax.rem(target, pair_chunks)
+        mine = columns(q, m, z_side)[...].reshape(n_slots, chunk_cols)
+        theirs = pair[q, m].reshape(n_slots, chunk_cols)
+        total = dot(acts[0], mine) + dot(acts[1], theirs)
+        term[target] = total.reshape(SUB, hidden // SUB, chunk_cols)
 
     def z_send(way, s, i):
         send(
@@ -316,7 +390,7 @@
         return zin[way, s, i].astype(F32)
 
     def z_step(s):
-        targets = (z_at(half_z - s), z_at(s - half_z))
+        targets = (pair_at(half_z - s), pair_at(s - half_z))
         for j in range(SUB if s > 0 else SUB // 2):
             early = j < SUB // 2
             for way in range(2):
@@ -329,88 +403,105 @@
 
     def z_finish():
         for i in range(SUB):
-            total = term[z, i] + z_arrive(0, half_z - 1, i) + z_arrive(1, half_z - 1, i)
+            total = term[place_z, i] + z_arrive(0, half_z - 1, i) + z_arrive(1, half_z - 1, i)
             rows_here = hidden // SUB
-            gd_ref[pl.ds(i * rows_here, rows_here), :] = (total * (1.0 / n_z)).astype(BF16)
+            gd_out[pl.ds(i * rows_here, rows_here), :] = (total * (1.0 / n_z)).astype(BF16)
+        store = pltpu.make_async_copy(gd_out, gd_hbm, out_sem.at[2])
+        store.start()
+        stores.append(store)
+
+    def gate_up(q):
+        block = row_block(0, q)
+        return dot_t(block, weight(gw, q)), dot_t(block, weight(uw, q))
+
+    def act_grad(q):
+        return dot_t(row_block(1, q), weight(dw, q))
+
+    def down_part(q):
+        put_part(0, q, dot(act_b, weight(dw, q)))
+
+    def input_part(q):
+        put_part(1, q, dot(gate_back, weight(gw, q)) + dot(up_back, weight(uw, q)))
 
     dispatch(0)
     dispatch(1)
     dispatch_wait(0)
-    gather_start(0)
+    gather_start(0, 0)
+    gather_start(0, 1)
     loads[0].wait()
     loads[1].wait()
-    block = row_block(0, x)
-    gate_s[...] = dot_t(block, weight(gw, x))
-    up_s[...] = dot_t(block, weight(uw, x))
+    gate_s[...], up_s[...] = gate_up(x)
     dispatch_wait(1)
-    gather_start(1)
+    gather_start(1, 0)
     gather_relay(0)
+    gather_start(1, 1)
+    pair_send(x)
     gather_near(0)
     for q in (left, right):
-        block = row_block(0, q)
-        gate_s[...] += dot_t(block, weight(gw, q))
-        up_s[...] += dot_t(block, weight(uw, q))
+        gate, up = gate_up(q)
+        gate_s[...] += gate
+        up_s[...] += up
+    gather_relay(1)
     gather_far(0)
-    block = row_block(0, far)
-    gate = gate_s[...] + dot_t(block, weight(gw, far))
-    up = up_s[...] + dot_t(block, weight(uw, far))
+    gate, up = gate_up(far)
+    gate = gate_s[...] + gate
+    up = up_s[...] + up
     squash = 1.0 / (1.0 + jnp.exp(-gate))
     swish = gate * squash
     act = swish * up
     gate_s[...] = up * squash * (1.0 + gate * (1.0 - squash))
     up_s[...] = swish
     act_b = act.astype(BF16)
-    act_t = act.T.astype(BF16)
+    acts[0] = act.T.astype(BF16)
+    act_send()
     loads[2].wait()
-    gather_relay(1)
-    put_part(0, far, dot(act_b, weight(dw, far)))
+    gather_near(1)
+    pair_send(left)
+    pair_send(right)
+    down_part(far)
     reduce_far(0)
-    for q in (right, left):
-        put_part(0, q, dot(act_b, weight(dw, q)))
+    down_part(right)
+    down_part(left)
     reduce_near(0)
-    put_part(0, x, dot(act_b, weight(dw, x)))
-    gather_near(1)
+    grad = act_grad(x) + act_grad(left) + act_grad(right)
     gather_far(1)
-    chunk_cols = term.shape[3]
-    per_quarter = q_cols // chunk_cols
-    for q in range(n_x):
-        block = dot(act_t, row_block(1, q))
-        for c in range(per_quarter):
-            piece = block[:, c * chunk_cols : (c + 1) * chunk_cols]
-            term[q * per_quarter + c] = piece.reshape(SUB, hidden // SUB, chunk_cols)
-    z_step(0)
-    reduce_relay(0)
-    grad = None
-    for q in range(n_x):
-        piece = dot_t(row_block(1, q), weight(dw, q))
-        grad = piece if grad is None else grad + piece
+    pair_send(far)
+    grad = grad + act_grad(far)
     gate_back = (grad * gate_s[...]).astype(BF16)
     up_back = (grad * up_s[...]).astype(BF16)
-    z_step(1)
-
-    def input_part(q):
-        put_part(1, q, dot(gate_back, weight(gw, q)) + dot(up_back, weight(uw, q)))
-
     input_part(far)
     reduce_far(1)
+    down_part(x)
+    reduce_relay(0)
+    act_arrive()
+    for q in (x, left, right, far):
+        pair_arrive(q)
+    make_term(pair_at(half_z))
+    z_step(0)
+    make_term(pair_at(half_z - 1))
+    make_term(pair_at(1 - half_z))
     input_part(right)
     input_part(left)
     reduce_near(1)
+    z_step(1)
+    for s in range(2, half_z):
+        make_term(pair_at(half_z - s))
+        make_term(pair_at(s - half_z))
+    make_term(place_z)
     reduce_end(0)
-    z_step(2)
     input_part(x)
     reduce_relay(1)
-    z_step(3)
+    z_step(2)
     reduce_end(1)
     combine(0)
-    z_step(4)
-    z_step(5)
+    for s in range(3, half_z):
+        z_step(s)
     combine(1)
-    finish(0, lo_ref)
-    z_step(6)
-    finish(1, gt_ref)
-    z_step(7)
     z_finish()
+    finish(0)
+    finish(1)
+    for store in stores:
+        store.wait()
     for copy in started:
         copy.wait_send()
 
@@ -425,9 +516,10 @@
     hidden = gate_weight.shape[2]
     q_cols = width // n_x
     n_slots = n_e * cap
-    half_e, half_z = n_e // 2, n_z // 2
+    half_e, n_pairs = n_e // 2, n_z // 2
+    half_z = n_pairs // 2
+    pair_chunks = n_pairs // n_x
     z_rows = width // n_z
-    vmem = pl.BlockSpec(memory_space=pltpu.VMEM)
     hbm = pl.BlockSpec(memory_space=pl.ANY)
     dma = pltpu.SemaphoreType.DMA
     weights = [jnp.swapaxes(w[0], 0, 1) for w in (gate_weight, up_weight, down_weight)]
@@ -440,9 +532,10 @@
             jax.ShapeDtypeStruct((tokens_here, width), BF16),
             jax.ShapeDtypeStruct((hidden, z_rows), BF16),
         ),
-        in_specs=[vmem] * 5 + [hbm] * 3,
-        out_specs=(vmem, vmem, vmem),
-        scratch_shapes=[pltpu.VMEM((hidden, width), BF16)] * 3
+        in_specs=[hbm] * 8,
+        out_specs=(hbm, hbm, hbm),
+        scratch_shapes=[pltpu.VMEM(v.shape, v.dtype) for v in (tokens, cotangent, *plans)]
+        + [pltpu.VMEM((hidden, width), BF16)] * 3
         + [
             pltpu.VMEM((2, n_x, tokens_here, q_cols), BF16),
             pltpu.VMEM((group_size, q_cols), F32),
@@ -457,10 +550,14 @@
             pltpu.VMEM((2, 2) + quarter, BF16),
             pltpu.VMEM((2, 2) + quarter, BF16),
             pltpu.VMEM((2, n_x, tokens_here, q_cols), BF16),
-            pltpu.VMEM((2, n_x, tokens_here, q_cols), BF16),
-            pltpu.VMEM((n_z, SUB, hidden // SUB, z_rows), F32),
+            pltpu.VMEM((2, hidden, n_slots), BF16),
+            pltpu.VMEM((n_x, pair_chunks, 2, half_e, cap, z_rows), BF16),
+            pltpu.VMEM((n_pairs, SUB, hidden // SUB, z_rows), F32),
             pltpu.VMEM((2, half_z, SUB, hidden // SUB, z_rows), BF16),
             pltpu.VMEM((2, half_z, SUB, hidden // SUB, z_rows), BF16),
+            pltpu.VMEM((hidden, z_rows), BF16),
+            dma((5,)),
+            dma((3,)),
             dma((3,)),
             dma((2, n_x)),
             dma((2, n_x)),
@@ -474,6 +571,10 @@
             dma((2, n_e)),
             dma((2, n_x)),
             dma((2, n_x)),
+            dma((1,)),
+            dma((1,)),
+            dma((n_x, pair_chunks)),
+            dma((n_x, pair_chunks)),
             dma((2, half_z, SUB)),
             dma((2, half_z, SUB)),
         ],

time: 80 us -> 73.8 us (0.922)
  Pallas kernels: 78.5 us -> 72.9 us
    pallas_call x1, Pallas kernels: 76.9 us -> 71.4 us  [shards(): pl.pallas_call(functools.partial(kernel, n_z, n_e), out_shape=(jax.ShapeD...]
where the time goes in v3:
time: 73.8 us; the launch traced here: 73.6 us
  Pallas kernels  72.9 us (99%)
    pallas_call x1, Pallas kernels, shards(): pl.pallas_call(functools.partial(kernel, n_z, n_e), out_shape=(jax.ShapeD...  71.4 us
    pallas_call x1, Pallas kernels, body(): pl.pallas_call(place, out_shape=tuple((jax.ShapeDtypeStruct(r.shape, r.dt...  1.58 us

profile of v3, /device:TPU:1, one launch (start us, length us, event | category | flops | bytes accessed | tf_op | source)
XLA Modules:
  0.0 73.6 jit_solution(5402040572687548605)
XLA Ops:
  0.6 71.4 %shard_map.103 = (bf16[4,2048]{1,0:T(4,128)(2,1)}, bf16[4,2048]{1,0:T(4,128)(2,1)}, bf16[352,128]{1,0:T(8,128)(2,1)}) custom-call(bf16[4,2048]{1,0:T(4,128)(2,1)} %tok_hbm.1, bf16[4,2048]{1,0:T(4,128)(2,1)} %cot_hbm.1, s32[6,16]{1,0:T(8,128)} %bitcast.18, s32[6,16]{1,0:T(8,128)} %bitcast.19, f32[6,16]{1,0:T(8,128)} %bitcast.20, bf16[352,2048]{1,0:T(8,128)(2,1)} %bitcast.15, ...), custom_call_target="tpu_custom_call" | custom-call | tf_op jit(solution)/shard_map/pallas_call | solution.py:528
  72.0 1.6 %shard_map.104 = (bf16[4,2048]{1,0:T(4,128)(2,1)}, bf16[4,2048]{1,0:T(4,128)(2,1)}, bf16[352,128]{1,0:T(8,128)(2,1)}) custom-call(bf16[4,2048]{1,0:T(4,128)(2,1)} %get-tuple-element.9.refs_0_, bf16[4,2048]{1,0:T(4,128)(2,1)} %get-tuple-element.10.refs_1_, bf16[352,128]{1,0:T(8,128)(2,1)} %get-tuple-element.11.refs_2_), custom_call_target="tpu_custom_call" | custom-call | tf_op jit(solution)/shard_map/pallas_call | solution.py:595

commit v4 on v3

--- a/solution.py
+++ b/solution.py
@@ -11,6 +11,8 @@
 F32 = jnp.float32
 BF16 = jnp.bfloat16
 SUB = 4
+UP_SUB = SUB // 2
+PIECES = 4
 
 
 def dot(left, right):
@@ -88,7 +90,7 @@
     tokens_here = tok_ref.shape[0]
     group_size = routes_ref.shape[1]
     n_slots = n_e * cap
-    half_e = n_e // 2
+    per_piece = n_e // PIECES
     n_pairs = n_z // 2
     half_z = n_pairs // 2
     hidden = gate_s.shape[1]
@@ -199,6 +201,11 @@
     placed_back = placed.T.astype(BF16)
     weighted_back = pieces(weighted.T)
 
+    near_first = [d for k in range(1, n_e // 2 + 1) for d in sorted({k, n_e - k})]
+
+    def rows_at(a, q, r):
+        return rows.at[a, q, r // per_piece, r % per_piece]
+
     def dispatch(a):
         for d in range(1, n_x):
             src = x_at(-d)
@@ -210,49 +217,64 @@
             slots = dot(placed_in, here)
         else:
             slots = dot(weighted_in[0], here) + dot(weighted_in[1], here)
-        dsend[a] = slots.reshape(n_e, cap, q_cols).astype(BF16).reshape(2, half_e, cap, q_cols)
-        for d in range(1, n_e):
+        dsend[a] = slots.reshape(n_e, cap, q_cols).astype(BF16)
+        for d in near_first:
             to = e_at(d)
             send(
-                dsend.at[a, to // half_e, lax.rem(to, half_e)],
-                rows.at[a, x, e // half_e, lax.rem(e, half_e)],
+                dsend.at[a, to],
+                rows_at(a, x, n_e - d),
                 sd_sem.at[a, d],
                 rd_sem.at[a, d],
                 {"expert": to},
             )
-        rows[a, x, e // half_e, lax.rem(e, half_e)] = dsend[a, e // half_e, lax.rem(e, half_e)]
-
-    def dispatch_wait(a):
-        for d in range(1, n_e):
-            src = e_at(-d)
-            arrive(
-                rows.at[a, x, src // half_e, lax.rem(src, half_e)],
-                sd_sem.at[a, d],
-                rd_sem.at[a, d],
-                {"expert": src},
-            )
+        rows[a, x, 0, 0] = dsend[a, e]
+
+    def dispatch_wait(a, p):
+        for r in range(max(1, p * per_piece), (p + 1) * per_piece):
+            d = n_e - r
+            arrive(rows_at(a, x, r), sd_sem.at[a, d], rd_sem.at[a, d], {"expert": e_at(r)})
 
     right, left = x_at(1), x_at(-1)
     far = x_at(2)
 
-    def gather_start(a, h):
-        g = 1 - h
-        send(rows.at[a, x, h], rows.at[a, x, h], sg_sem.at[a, 0, h], rg_sem.at[a, 0, h], {"tensor": right})
-        send(rows.at[a, x, g], rows.at[a, x, g], sg_sem.at[a, 1, g], rg_sem.at[a, 1, g], {"tensor": left})
-
-    def gather_relay(a):
-        arrive(rows.at[a, left, 0], sg_sem.at[a, 0, 0], rg_sem.at[a, 0, 0], {"tensor": left})
-        send(rows.at[a, left, 0], rows.at[a, left, 0], sg_sem.at[a, 2, 0], rg_sem.at[a, 2, 0], {"tensor": right})
-        arrive(rows.at[a, right, 1], sg_sem.at[a, 1, 1], rg_sem.at[a, 1, 1], {"tensor": right})
-        send(rows.at[a, right, 1], rows.at[a, right, 1], sg_sem.at[a, 2, 1], rg_sem.at[a, 2, 1], {"tensor": left})
+    def gathered(a, q, p):
+        return rows.at[a, q, p] if a < 2 else pair.at[q, :, p]
+
+    def gather_send(a, q, p, to, way, hop):
+        ref = gathered(a, q, p)
+        send(ref, ref, sg_sem.at[a, way, hop, p], rg_sem.at[a, way, hop, p], {"tensor": to})
+
+    def gather_wait(a, q, p, way, hop):
+        origin = left if way == 0 else right
+        arrive(gathered(a, q, p), sg_sem.at[a, way, hop, p], rg_sem.at[a, way, hop, p], {"tensor": origin})
+
+    relay_right, relay_left = (0, 1), (3, 2)
+
+    def gather_start(a, k):
+        gather_send(a, x, relay_right[k], right, 0, 0)
+        gather_send(a, x, relay_left[k], left, 1, 0)
+
+    def gather_rest(a, k):
+        gather_send(a, x, relay_left[k], right, 0, 0)
+        gather_send(a, x, relay_right[k], left, 1, 0)
+
+    def gather_relay(a, k):
+        p = relay_right[k]
+        gather_wait(a, left, p, 0, 0)
+        gather_send(a, left, p, right, 0, 1)
+        p = relay_left[k]
+        gather_wait(a, right, p, 1, 0)
+        gather_send(a, right, p, left, 1, 1)
 
     def gather_near(a):
-        arrive(rows.at[a, left, 1], sg_sem.at[a, 0, 1], rg_sem.at[a, 0, 1], {"tensor": left})
-        arrive(rows.at[a, right, 0], sg_sem.at[a, 1, 0], rg_sem.at[a, 1, 0], {"tensor": right})
+        for k in range(2):
+            gather_wait(a, left, relay_left[k], 0, 0)
+            gather_wait(a, right, relay_right[k], 1, 0)
 
     def gather_far(a):
-        arrive(rows.at[a, far, 0], sg_sem.at[a, 2, 0], rg_sem.at[a, 2, 0], {"tensor": left})
-        arrive(rows.at[a, far, 1], sg_sem.at[a, 2, 1], rg_sem.at[a, 2, 1], {"tensor": right})
+        for k in range(2):
+            gather_wait(a, far, relay_right[k], 0, 1)
+            gather_wait(a, far, relay_left[k], 1, 1)
 
     def weight(ref, q):
         return ref[:, pl.ds(pl.multiple_of(q * q_cols, q_cols), q_cols)]
@@ -261,41 +283,56 @@
         return rows[a, q].reshape(n_slots, q_cols)
 
     def put_part(b, q, value):
-        part[b, q] = value.reshape(n_e, cap, q_cols).astype(BF16).reshape(2, half_e, cap, q_cols)
+        part[b, q] = value.reshape(n_e, cap, q_cols).astype(BF16).reshape(PIECES, per_piece, cap, q_cols)
+
+    def reduce_send(b, src, dst, way, hop, p):
+        to = right if way == 0 else left
+        send(src, dst, sr_sem.at[b, way, hop, p], rr_sem.at[b, way, hop, p], {"tensor": to})
+
+    def reduce_wait(b, dst, way, hop, p):
+        origin = left if way == 0 else right
+        arrive(dst, sr_sem.at[b, way, hop, p], rr_sem.at[b, way, hop, p], {"tensor": origin})
 
     def reduce_far(b):
-        send(part.at[b, far, 0], rs_far.at[b, 0], sr_sem.at[b, 0], rr_sem.at[b, 0], {"tensor": right})
-        send(part.at[b, far, 1], rs_far.at[b, 1], sr_sem.at[b, 1], rr_sem.at[b, 1], {"tensor": left})
+        for k in range(2):
+            p = relay_right[k]
+            reduce_send(b, part.at[b, far, p], rs_far.at[b, p], 0, 0, p)
+            p = relay_left[k]
+            reduce_send(b, part.at[b, far, p], rs_far.at[b, p], 1, 0, p)
 
     def reduce_near(b):
-        send(part.at[b, right, 1], rs_near.at[b, 0, 1], sr_sem.at[b, 2], rr_sem.at[b, 2], {"tensor": right})
-        send(part.at[b, left, 0], rs_near.at[b, 1, 0], sr_sem.at[b, 3], rr_sem.at[b, 3], {"tensor": left})
+        for k in range(2):
+            p = relay_left[k]
+            reduce_send(b, part.at[b, right, p], rs_near.at[b, 0, p], 0, 1, p)
+            p = relay_right[k]
+            reduce_send(b, part.at[b, left, p], rs_near.at[b, 1, p], 1, 1, p)
 
     def reduce_relay(b):
-        arrive(rs_far.at[b, 0], sr_sem.at[b, 0], rr_sem.at[b, 0], {"tensor": left})
-        rs_sum[b, 0] = (rs_far[b, 0].astype(F32) + part[b, right, 0].astype(F32)).astype(BF16)
-        send(rs_sum.at[b, 0], rs_near.at[b, 0, 0], sr_sem.at[b, 4], rr_sem.at[b, 4], {"tensor": right})
-        arrive(rs_far.at[b, 1], sr_sem.at[b, 1], rr_sem.at[b, 1], {"tensor": right})
-        rs_sum[b, 1] = (rs_far[b, 1].astype(F32) + part[b, left, 1].astype(F32)).astype(BF16)
-        send(rs_sum.at[b, 1], rs_near.at[b, 1, 1], sr_sem.at[b, 5], rr_sem.at[b, 5], {"tensor": left})
+        for k in range(2):
+            for way, p in ((0, relay_right[k]), (1, relay_left[k])):
+                onward = right if way == 0 else left
+                reduce_wait(b, rs_far.at[b, p], way, 0, p)
+                rs_sum[b, p] = (rs_far[b, p].astype(F32) + part[b, onward, p].astype(F32)).astype(BF16)
+                reduce_send(b, rs_sum.at[b, p], rs_near.at[b, way, p], way, 1, p)
 
     def reduce_end(b):
-        arrive(rs_near.at[b, 0, 1], sr_sem.at[b, 2], rr_sem.at[b, 2], {"tensor": left})
-        arrive(rs_near.at[b, 1, 0], sr_sem.at[b, 3], rr_sem.at[b, 3], {"tensor": right})
-        arrive(rs_near.at[b, 0, 0], sr_sem.at[b, 4], rr_sem.at[b, 4], {"tensor": left})
-        arrive(rs_near.at[b, 1, 1], sr_sem.at[b, 5], rr_sem.at[b, 5], {"tensor": right})
-        total = part[b, x].astype(F32) + rs_near[b, 0].astype(F32) + rs_near[b, 1].astype(F32)
-        ysend[b] = total.astype(BF16)
-        for d in range(1, n_e):
-            to = e_at(d)
-            send(
-                ysend.at[b, to // half_e, lax.rem(to, half_e)],
-                yret.at[b, e // half_e, lax.rem(e, half_e)],
-                sy_sem.at[b, d],
-                ry_sem.at[b, d],
-                {"expert": to},
-            )
-        yret[b, e // half_e, lax.rem(e, half_e)] = ysend[b, e // half_e, lax.rem(e, half_e)]
+        for p in (0, 3, 1, 2):
+            for way in range(2):
+                reduce_wait(b, rs_near.at[b, way, p], way, 1, p)
+            total = part[b, x, p].astype(F32) + rs_near[b, 0, p].astype(F32) + rs_near[b, 1, p].astype(F32)
+            ysend[b, p] = total.astype(BF16)
+            for i in range(per_piece):
+                r = p * per_piece + i
+                if r == 0:
+                    yret[b, e] = ysend[b, 0, 0]
+                    continue
+                send(
+                    ysend.at[b, p, i],
+                    yret.at[b, e],
+                    sy_sem.at[b, r],
+                    ry_sem.at[b, r],
+                    {"expert": e_at(r)},
+                )
 
     stores = []
     results = (lo_hbm, gt_hbm)
@@ -306,12 +343,7 @@
     def combine(b):
         for d in range(1, n_e):
             src = e_at(-d)
-            arrive(
-                yret.at[b, src // half_e, lax.rem(src, half_e)],
-                sy_sem.at[b, d],
-                ry_sem.at[b, d],
-                {"expert": src},
-            )
+            arrive(yret.at[b, src], sy_sem.at[b, d], ry_sem.at[b, d], {"expert": src})
         slots = yret[b].reshape(n_slots, q_cols)
         if b == 0:
             mixed = dot(weighted_back[0], slots) + dot(weighted_back[1], slots)
@@ -345,19 +377,13 @@
         start = pl.multiple_of((2 * m + side) * chunk_cols, chunk_cols)
         return rows.at[1, q, :, :, :, pl.ds(start, chunk_cols)]
 
-    def pair_send(q):
+    def pair_send():
         for m in range(pair_chunks):
-            send(
-                columns(q, m, 1 - z_side),
-                pair.at[q, m],
-                sp_sem.at[q, m],
-                rp_sem.at[q, m],
-                {"dp": partner},
-            )
-
-    def pair_arrive(q):
+            send(columns(x, m, 1 - z_side), pair.at[x, m], sp_sem.at[m], rp_sem.at[m], {"dp": partner})
+
+    def pair_arrive():
         for m in range(pair_chunks):
-            arrive(pair.at[q, m], sp_sem.at[q, m], rp_sem.at[q, m], {"dp": partner})
+            arrive(pair.at[x, m], sp_sem.at[m], rp_sem.at[m], {"dp": partner})
 
     place_z = z // 2
 
@@ -389,12 +415,14 @@
         )
         return zin[way, s, i].astype(F32)
 
-    def z_step(s):
+    def z_step(s, first):
         targets = (pair_at(half_z - s), pair_at(s - half_z))
-        for j in range(SUB if s > 0 else SUB // 2):
-            early = j < SUB // 2
+        for j in range(SUB):
             for way in range(2):
                 i = j if way == 0 else SUB - 1 - j
+                early = j < (UP_SUB if way == 0 else SUB - UP_SUB)
+                if early != first:
+                    continue
                 value = term[targets[way], i]
                 if s > 1 or (s == 1 and early):
                     value = value + z_arrive(way, s - 1, i)
@@ -425,23 +453,36 @@
 
     dispatch(0)
     dispatch(1)
-    dispatch_wait(0)
-    gather_start(0, 0)
-    gather_start(0, 1)
+    for k in range(2):
+        dispatch_wait(0, relay_right[k])
+        dispatch_wait(0, relay_left[k])
+        gather_start(0, k)
+    gather_rest(0, 0)
+    gather_rest(0, 1)
     loads[0].wait()
     loads[1].wait()
     gate_s[...], up_s[...] = gate_up(x)
-    dispatch_wait(1)
-    gather_start(1, 0)
-    gather_relay(0)
-    gather_start(1, 1)
-    pair_send(x)
+    for k in range(2):
+        dispatch_wait(1, relay_right[k])
+        dispatch_wait(1, relay_left[k])
+        gather_start(1, k)
+    pair_send()
+    gather_relay(0, 0)
+    gather_relay(0, 1)
+    gather_rest(1, 0)
+    gather_rest(1, 1)
     gather_near(0)
     for q in (left, right):
         gate, up = gate_up(q)
         gate_s[...] += gate
         up_s[...] += up
-    gather_relay(1)
+    gather_relay(1, 0)
+    gather_relay(1, 1)
+    pair_arrive()
+    gather_start(2, 0)
+    gather_start(2, 1)
+    gather_rest(2, 0)
+    gather_rest(2, 1)
     gather_far(0)
     gate, up = gate_up(far)
     gate = gate_s[...] + gate
@@ -456,50 +497,51 @@
     act_send()
     loads[2].wait()
     gather_near(1)
-    pair_send(left)
-    pair_send(right)
     down_part(far)
     reduce_far(0)
     down_part(right)
     down_part(left)
+    gather_relay(2, 0)
+    gather_relay(2, 1)
     reduce_near(0)
     grad = act_grad(x) + act_grad(left) + act_grad(right)
     gather_far(1)
-    pair_send(far)
     grad = grad + act_grad(far)
     gate_back = (grad * gate_s[...]).astype(BF16)
     up_back = (grad * up_s[...]).astype(BF16)
     input_part(far)
     reduce_far(1)
-    down_part(x)
-    reduce_relay(0)
     act_arrive()
-    for q in (x, left, right, far):
-        pair_arrive(q)
+    gather_near(2)
+    gather_far(2)
     make_term(pair_at(half_z))
-    z_step(0)
+    z_step(0, True)
     make_term(pair_at(half_z - 1))
     make_term(pair_at(1 - half_z))
+    z_step(1, False)
+    reduce_relay(0)
     input_part(right)
     input_part(left)
     reduce_near(1)
-    z_step(1)
     for s in range(2, half_z):
         make_term(pair_at(half_z - s))
         make_term(pair_at(s - half_z))
     make_term(place_z)
-    reduce_end(0)
+    down_part(x)
     input_part(x)
     reduce_relay(1)
-    z_step(2)
+    reduce_end(0)
+    z_step(1, True)
+    z_step(2, False)
     reduce_end(1)
+    z_step(2, True)
     combine(0)
-    for s in range(3, half_z):
-        z_step(s)
+    z_step(3, False)
     combine(1)
-    z_finish()
+    z_step(3, True)
     finish(0)
     finish(1)
+    z_finish()
     for store in stores:
         store.wait()
     for copy in started:
@@ -516,7 +558,7 @@
     hidden = gate_weight.shape[2]
     q_cols = width // n_x
     n_slots = n_e * cap
-    half_e, n_pairs = n_e // 2, n_z // 2
+    per_piece, n_pairs = n_e // PIECES, n_z // 2
     half_z = n_pairs // 2
     pair_chunks = n_pairs // n_x
     z_rows = width // n_z
@@ -524,7 +566,8 @@
     dma = pltpu.SemaphoreType.DMA
     weights = [jnp.swapaxes(w[0], 0, 1) for w in (gate_weight, up_weight, down_weight)]
     plans = [v.T for v in (routes, positions, combine_weights)]
-    quarter = (half_e, cap, q_cols)
+    quarter = (PIECES, per_piece, cap, q_cols)
+    slots = (n_e, cap, q_cols)
     return pl.pallas_call(
         functools.partial(kernel, n_z, n_e),
         out_shape=(
@@ -539,19 +582,19 @@
         + [
             pltpu.VMEM((2, n_x, tokens_here, q_cols), BF16),
             pltpu.VMEM((group_size, q_cols), F32),
-            pltpu.VMEM((2, 2) + quarter, BF16),
-            pltpu.VMEM((2, n_x, 2) + quarter, BF16),
+            pltpu.VMEM((2,) + slots, BF16),
+            pltpu.VMEM((2, n_x) + quarter, BF16),
             pltpu.VMEM((n_slots, hidden), F32),
             pltpu.VMEM((n_slots, hidden), F32),
-            pltpu.VMEM((2, n_x, 2) + quarter, BF16),
+            pltpu.VMEM((2, n_x) + quarter, BF16),
+            pltpu.VMEM((2,) + quarter, BF16),
+            pltpu.VMEM((2,) + quarter, BF16),
             pltpu.VMEM((2, 2) + quarter, BF16),
-            pltpu.VMEM((2, 2) + quarter, BF16),
-            pltpu.VMEM((2, 2, 2) + quarter, BF16),
-            pltpu.VMEM((2, 2) + quarter, BF16),
-            pltpu.VMEM((2, 2) + quarter, BF16),
+            pltpu.VMEM((2,) + quarter, BF16),
+            pltpu.VMEM((2,) + slots, BF16),
             pltpu.VMEM((2, n_x, tokens_here, q_cols), BF16),
             pltpu.VMEM((2, hidden, n_slots), BF16),
-            pltpu.VMEM((n_x, pair_chunks, 2, half_e, cap, z_rows), BF16),
+            pltpu.VMEM((n_x, pair_chunks, PIECES, per_piece, cap, z_rows), BF16),
             pltpu.VMEM((n_pairs, SUB, hidden // SUB, z_rows), F32),
             pltpu.VMEM((2, half_z, SUB, hidden // SUB, z_rows), BF16),
             pltpu.VMEM((2, half_z, SUB, hidden // SUB, z_rows), BF16),
@@ -563,18 +606,18 @@
             dma((2, n_x)),
             dma((2, n_e)),
             dma((2, n_e)),
-            dma((2, 3, 2)),
-            dma((2, 3, 2)),
-            dma((2, 6)),
-            dma((2, 6)),
+            dma((3, 2, 2, PIECES)),
+            dma((3, 2, 2, PIECES)),
+            dma((2, 2, 2, PIECES)),
+            dma((2, 2, 2, PIECES)),
             dma((2, n_e)),
             dma((2, n_e)),
             dma((2, n_x)),
             dma((2, n_x)),
             dma((1,)),
             dma((1,)),
-            dma((n_x, pair_chunks)),
-            dma((n_x, pair_chunks)),
+            dma((pair_chunks,)),
+            dma((pair_chunks,)),
             dma((2, half_z, SUB)),
             dma((2, half_z, SUB)),
         ],

time: 73.8 us -> 71 us (0.962)
  Pallas kernels: 72.9 us -> 70.2 us
    pallas_call x1, Pallas kernels: 71.4 us -> 68.6 us  [shards(): pl.pallas_call(functools.partial(kernel, n_z, n_e), out_shape=(jax.ShapeD...]
where the time goes in v4:
time: 71 us; the launch traced here: 70.8 us
  Pallas kernels  70.2 us (99%)
    pallas_call x1, Pallas kernels, shards(): pl.pallas_call(functools.partial(kernel, n_z, n_e), out_shape=(jax.ShapeD...  68.6 us
    pallas_call x1, Pallas kernels, body(): pl.pallas_call(place, out_shape=tuple((jax.ShapeDtypeStruct(r.shape, r.dt...  1.58 us

profile of v4, /device:TPU:1, one launch (start us, length us, event | category | flops | bytes accessed | tf_op | source)
XLA Modules:
  0.0 70.8 jit_solution(9977125088668553249)
XLA Ops:
  0.6 68.6 %shard_map.103 = (bf16[4,2048]{1,0:T(4,128)(2,1)}, bf16[4,2048]{1,0:T(4,128)(2,1)}, bf16[352,128]{1,0:T(8,128)(2,1)}) custom-call(bf16[4,2048]{1,0:T(4,128)(2,1)} %tok_hbm.1, bf16[4,2048]{1,0:T(4,128)(2,1)} %cot_hbm.1, s32[6,16]{1,0:T(8,128)} %bitcast.18, s32[6,16]{1,0:T(8,128)} %bitcast.19, f32[6,16]{1,0:T(8,128)} %bitcast.20, bf16[352,2048]{1,0:T(8,128)(2,1)} %bitcast.15, ...), custom_call_target="tpu_custom_call" | custom-call | tf_op jit(solution)/shard_map/pallas_call | solution.py:571
  69.2 1.6 %shard_map.104 = (bf16[4,2048]{1,0:T(4,128)(2,1)}, bf16[4,2048]{1,0:T(4,128)(2,1)}, bf16[352,128]{1,0:T(8,128)(2,1)}) custom-call(bf16[4,2048]{1,0:T(4,128)(2,1)} %get-tuple-element.9.refs_0_, bf16[4,2048]{1,0:T(4,128)(2,1)} %get-tuple-element.10.refs_1_, bf16[352,128]{1,0:T(8,128)(2,1)} %get-tuple-element.11.refs_2_), custom_call_target="tpu_custom_call" | custom-call | tf_op jit(solution)/shard_map/pallas_call | solution.py:638

commit v5 on v4

--- a/solution.py
+++ b/solution.py
@@ -10,7 +10,7 @@
 MESH = pl.DeviceIdType.MESH
 F32 = jnp.float32
 BF16 = jnp.bfloat16
-SUB = 4
+SUB = 2
 UP_SUB = SUB // 2
 PIECES = 4
 
@@ -433,10 +433,11 @@
         for i in range(SUB):
             total = term[place_z, i] + z_arrive(0, half_z - 1, i) + z_arrive(1, half_z - 1, i)
             rows_here = hidden // SUB
-            gd_out[pl.ds(i * rows_here, rows_here), :] = (total * (1.0 / n_z)).astype(BF16)
-        store = pltpu.make_async_copy(gd_out, gd_hbm, out_sem.at[2])
-        store.start()
-        stores.append(store)
+            here = pl.ds(i * rows_here, rows_here)
+            gd_out[here, :] = (total * (1.0 / n_z)).astype(BF16)
+            store = pltpu.make_async_copy(gd_out.at[here, :], gd_hbm.at[here, :], out_sem.at[2 + i])
+            store.start()
+            stores.append(store)
 
     def gate_up(q):
         block = row_block(0, q)
@@ -600,7 +601,7 @@
             pltpu.VMEM((2, half_z, SUB, hidden // SUB, z_rows), BF16),
             pltpu.VMEM((hidden, z_rows), BF16),
             dma((5,)),
-            dma((3,)),
+            dma((2 + SUB,)),
             dma((3,)),
             dma((2, n_x)),
             dma((2, n_x)),

time: 71 us -> 70.8 us (level)
  no operation moved by 1% of the time
where the time goes in v5:
time: 70.8 us; the launch traced here: 70.6 us
  Pallas kernels  69.9 us (99%)
    pallas_call x1, Pallas kernels, shards(): pl.pallas_call(functools.partial(kernel, n_z, n_e), out_shape=(jax.ShapeD...  68.4 us
    pallas_call x1, Pallas kernels, body(): pl.pallas_call(place, out_shape=tuple((jax.ShapeDtypeStruct(r.shape, r.dt...  1.58 us

profile of v5, /device:TPU:1, one launch (start us, length us, event | category | flops | bytes accessed | tf_op | source)
XLA Modules:
  0.0 70.6 jit_solution(1824905795873047091)
XLA Ops:
  0.6 68.4 %shard_map.103 = (bf16[4,2048]{1,0:T(4,128)(2,1)}, bf16[4,2048]{1,0:T(4,128)(2,1)}, bf16[352,128]{1,0:T(8,128)(2,1)}) custom-call(bf16[4,2048]{1,0:T(4,128)(2,1)} %tok_hbm.1, bf16[4,2048]{1,0:T(4,128)(2,1)} %cot_hbm.1, s32[6,16]{1,0:T(8,128)} %bitcast.18, s32[6,16]{1,0:T(8,128)} %bitcast.19, f32[6,16]{1,0:T(8,128)} %bitcast.20, bf16[352,2048]{1,0:T(8,128)(2,1)} %bitcast.15, ...), custom_call_target="tpu_custom_call" | custom-call | tf_op jit(solution)/shard_map/pallas_call | solution.py:572
  69.0 1.6 %shard_map.104 = (bf16[4,2048]{1,0:T(4,128)(2,1)}, bf16[4,2048]{1,0:T(4,128)(2,1)}, bf16[352,128]{1,0:T(8,128)(2,1)}) custom-call(bf16[4,2048]{1,0:T(4,128)(2,1)} %get-tuple-element.9.refs_0_, bf16[4,2048]{1,0:T(4,128)(2,1)} %get-tuple-element.10.refs_1_, bf16[352,128]{1,0:T(8,128)(2,1)} %get-tuple-element.11.refs_2_), custom_call_target="tpu_custom_call" | custom-call | tf_op jit(solution)/shard_map/pallas_call | solution.py:639
